TPU v7x, 32 devices: a whole 2x2x4 slice. The times are simulated.
32 devices in a mesh: slab: 8 (over z, y), head: 4 (over x, core).
Axes of the slice: x: 2, y: 2, z: 4, core: 2. Of those that a mesh axis runs over, the one named last changes fastest.
Arguments:
- q_raw: bfloat16 [3072, 2560], P('slab', 'head'), may hold values from -64 to 64
- k_raw: bfloat16 [12288, 2560], P('slab', 'head'), may hold values from -64 to 64
- values: bfloat16 [12288, 2560], P('slab', 'head'), may hold values from -6 to 6
- q_gain: float32 [2560], P('head'), may hold values from 0.5 to 1.5
- k_gain: float32 [2560], P('head'), may hold values from 0.5 to 1.5
- cotangent: bfloat16 [3072, 2560], P('slab', 'head'), may hold values from -6 to 6
- kept_tiles: int32 [48, 20, 12], P('slab', 'head'), may hold values from 0 to 191, as said below
Outputs:
- attn_out: bfloat16 [3072, 2560], P('slab', 'head')
- dq_normed: bfloat16 [3072, 2560], P('slab', 'head')
- dk_normed: bfloat16 [12288, 2560], P('slab', 'head')
- dv: bfloat16 [12288, 2560], P('slab', 'head')
Inputs may be any that keep to these rules, and one draw needn't show every extreme that they name: kept_tiles[i, h, :] names 12 distinct key tiles. Query tile i is key tile 4 i; slab d holds query tiles d * 6 to (d + 1) * 6 - 1 and key tiles d * 24 to (d + 1) * 24 - 1. The first 10 entries lie in the query's own slab, the first of all being tile 4 i; the last 2 lie in other slabs. Over all query tiles of one slab and the heads that one index of head holds, the kept tiles of any one other slab form at most 2 distinct (tile, head) pairs; in every draw some slab is kept 2 such pairs by every other slab.
All inputs are finite; a program needn't handle non-finite values.
Results may differ from a plain program's by a relative error of at most 0.012.
The roundings to bfloat16 on the way count: a program that leaves them out, or rounds other values in their place, can miss the bound.
Values may be sent and summed in bfloat16 or wider, within the bound.
No kernel may reach another device: no remote copies, remote signals or barrier semaphores. Data moves between devices by JAX's collectives and lax.ppermute only.
A program may use at most 128 MiB of HBM per device.

v0:
```python
import math

import jax
import jax.numpy as jnp
from jax import lax
from jax.sharding import PartitionSpec as P

TILE = 64
NEAR = 10
CAP = 2


NORM_EPSILON = 1e-06


def tile_scores(queries, kept_keys, score_scale):
    return (
        jnp.einsum("jqhd,jhkd->jhqk", queries, kept_keys, preferred_element_type=jnp.float32)
        * score_scale
    )


def flatten_kept(stacked):
    return stacked.reshape(stacked.shape[0], stacked.shape[1], -1, stacked.shape[-1])


def local(q_raw, k_raw, values, q_gain, k_gain, cotangent, kept_tiles):
    slab_count = lax.axis_size("slab")
    group_count = lax.axis_size("head")
    own_slab = lax.axis_index("slab")
    query_tiles, head_count, kept_count = kept_tiles.shape
    local_width = q_raw.shape[1]
    head_size = local_width // head_count
    key_tiles = k_raw.shape[0] // TILE
    full_width = local_width * group_count
    score_scale = 1.0 / math.sqrt(head_size)
    q_sum = jnp.sum(jnp.square(q_raw.astype(jnp.float32)), axis=1)
    k_sum = jnp.sum(jnp.square(k_raw.astype(jnp.float32)), axis=1)
    q_sum, k_sum = lax.psum((q_sum, k_sum), "head")
    q_normed = (
        q_raw.astype(jnp.float32) * lax.rsqrt(q_sum / full_width + NORM_EPSILON)[:, None] * q_gain
    ).astype(jnp.bfloat16)
    k_normed = (
        k_raw.astype(jnp.float32) * lax.rsqrt(k_sum / full_width + NORM_EPSILON)[:, None] * k_gain
    ).astype(jnp.bfloat16)
    key_table = k_normed.reshape(key_tiles, TILE, head_count, head_size)
    value_table = values.reshape(key_tiles, TILE, head_count, head_size)
    head_ids = jnp.arange(head_count, dtype=jnp.int32)[None, :, None]
    near_tiles = kept_tiles[:, :, :NEAR] - own_slab * key_tiles
    far_global = kept_tiles[:, :, NEAR:]
    far_owner = far_global // key_tiles
    pairs_per_owner = key_tiles * head_count
    flat_use = far_owner * pairs_per_owner + far_global % key_tiles * head_count + head_ids
    all_pairs = jnp.arange(slab_count * pairs_per_owner, dtype=jnp.int32)
    needed = jnp.any(flat_use.reshape(-1)[:, None] == all_pairs[None, :], axis=0).reshape(
        slab_count, pairs_per_owner
    )
    pair_rank = jnp.cumsum(needed.astype(jnp.int32), axis=1) - 1
    local_pairs = jnp.arange(pairs_per_owner, dtype=jnp.int32)
    slot_columns = []
    for slot_index in range(CAP):
        slot_hit = needed & (pair_rank == slot_index)
        slot_columns.append(jnp.sum(jnp.where(slot_hit, local_pairs[None, :], 0), axis=1))
    request = jnp.stack(slot_columns, axis=1)
    use_slot = far_owner * CAP + pair_rank.reshape(-1)[flat_use]
    blocks = query_tiles // 2

    def to_blocks(array):
        return array.reshape((blocks, 2) + array.shape[1:])

    q_blocks = to_blocks(q_normed.reshape(query_tiles, TILE, head_count, head_size))
    cot_blocks = to_blocks(cotangent.reshape(query_tiles, TILE, head_count, head_size))
    near_blocks = to_blocks(near_tiles)
    use_blocks = to_blocks(use_slot)
    wanted = lax.all_to_all(request, "slab", split_axis=0, concat_axis=0, tiled=True)
    send_tiles = wanted // head_count
    send_heads = wanted % head_count
    outgoing = (key_table[send_tiles, :, send_heads, :], value_table[send_tiles, :, send_heads, :])
    far_keys, far_values = (
        lax.all_to_all(outgoing[0], "slab", split_axis=0, concat_axis=0, tiled=True),
        lax.all_to_all(outgoing[1], "slab", split_axis=0, concat_axis=0, tiled=True),
    )
    fetched_keys = far_keys.reshape(slab_count * CAP, TILE, head_size)
    fetched_values = far_values.reshape(slab_count * CAP, TILE, head_size)

    def gather_kept(source_table, fetched_pool, near_block, use_block):
        joined = jnp.concatenate(
            (source_table[near_block, :, head_ids, :], fetched_pool[use_block]), axis=2
        )
        return flatten_kept(joined)

    def block_scores(queries, near_block, use_block):
        return tile_scores(
            queries, gather_kept(key_table, fetched_keys, near_block, use_block), score_scale
        )

    def forward_block(block_items):
        queries, near_block, use_block, earlier = block_items
        scores = block_scores(queries, near_block, use_block)
        row_max = jnp.max(scores, axis=-1, keepdims=True)
        log_total = row_max + jnp.log(jnp.sum(jnp.exp(scores - row_max), axis=-1, keepdims=True))
        attn_weights = jnp.exp(scores - log_total).astype(jnp.bfloat16)
        kept_values = gather_kept(value_table, fetched_values, near_block, use_block)
        attn_block = jnp.einsum(
            "jhqk,jhkd->jqhd", attn_weights, kept_values, preferred_element_type=jnp.float32
        ).astype(jnp.bfloat16)
        return (attn_block, log_total)

    result_panels, total_blocks = lax.map(
        forward_block, (q_blocks, near_blocks, use_blocks, near_blocks)
    )

    def backward_block(grad_carry, block_items):
        key_grad, value_grad, far_key_grad, far_value_grad = grad_carry
        queries, cot_block, attn_block, log_total, near_block, use_block = block_items
        kept_keys = gather_kept(key_table, fetched_keys, near_block, use_block)
        kept_values = gather_kept(value_table, fetched_values, near_block, use_block)
        scores = tile_scores(queries, kept_keys, score_scale)
        attn_weights = jnp.exp(scores - log_total).astype(jnp.bfloat16)
        row_delta = jnp.sum(cot_block.astype(jnp.float32) * attn_block.astype(jnp.float32), axis=-1)
        row_delta = jnp.swapaxes(row_delta, 1, 2)[..., None]
        grad_weights = jnp.einsum(
            "jqhd,jhkd->jhqk", cot_block, kept_values, preferred_element_type=jnp.float32
        )
        dscore = (
            attn_weights.astype(jnp.float32) * (grad_weights - row_delta) * score_scale
        ).astype(jnp.bfloat16)
        dquery = jnp.einsum(
            "jhqk,jhkd->jqhd", dscore, kept_keys, preferred_element_type=jnp.float32
        ).astype(jnp.bfloat16)
        grad_keys = jnp.einsum(
            "jhqk,jqhd->jhkd", dscore, queries, preferred_element_type=jnp.float32
        )
        grad_values = jnp.einsum(
            "jhqk,jqhd->jhkd", attn_weights, cot_block, preferred_element_type=jnp.float32
        )
        tile_shape = (grad_keys.shape[0], grad_keys.shape[1], kept_count, TILE, head_size)
        grad_keys = grad_keys.reshape(tile_shape)
        grad_values = grad_values.reshape(tile_shape)
        key_grad = key_grad.at[near_block, :, head_ids, :].add(grad_keys[:, :, :NEAR])
        value_grad = value_grad.at[near_block, :, head_ids, :].add(grad_values[:, :, :NEAR])
        far_key_grad = far_key_grad.at[use_block].add(grad_keys[:, :, NEAR:])
        far_value_grad = far_value_grad.at[use_block].add(grad_values[:, :, NEAR:])
        return ((key_grad, value_grad, far_key_grad, far_value_grad), dquery)

    local_zero = jnp.zeros((key_tiles, TILE, head_count, head_size), jnp.float32)
    far_zero = jnp.zeros((slab_count * CAP, TILE, head_size), jnp.float32)
    final_grads, dq_blocks = lax.scan(
        backward_block,
        (local_zero, local_zero, far_zero, far_zero),
        (q_blocks, cot_blocks, result_panels, total_blocks, near_blocks, use_blocks),
    )
    key_grad, value_grad, far_key_grad, far_value_grad = final_grads
    returned_keys, returned_values = (
        lax.all_to_all(
            far_key_grad.reshape(slab_count, CAP, TILE, head_size),
            "slab",
            split_axis=0,
            concat_axis=0,
            tiled=True,
        ),
        lax.all_to_all(
            far_value_grad.reshape(slab_count, CAP, TILE, head_size),
            "slab",
            split_axis=0,
            concat_axis=0,
            tiled=True,
        ),
    )
    key_grad = key_grad.at[send_tiles, :, send_heads, :].add(returned_keys)
    value_grad = value_grad.at[send_tiles, :, send_heads, :].add(returned_values)
    attn_out = result_panels.reshape(query_tiles * TILE, local_width)
    dq_normed = dq_blocks.reshape(query_tiles * TILE, local_width)
    dk_normed = key_grad.astype(jnp.bfloat16).reshape(key_tiles * TILE, local_width)
    dv_local = value_grad.astype(jnp.bfloat16).reshape(key_tiles * TILE, local_width)
    return (attn_out, dq_normed, dk_normed, dv_local)


def solution(mesh):
    return jax.shard_map(
        local,
        mesh=mesh,
        in_specs=(
            P("slab", "head"),
            P("slab", "head"),
            P("slab", "head"),
            P("head"),
            P("head"),
            P("slab", "head"),
            P("slab", "head", None),
        ),
        out_specs=(P("slab", "head"), P("slab", "head"), P("slab", "head"), P("slab", "head")),
        check_vma=False,
    )
```

profile of v0, /device:TPU:0, one launch (start us, length us, event | category | flops | bytes accessed | tf_op | source)
XLA Modules:
  0.0 379.9 jit_solution(4042738416946943885)
XLA Ops:
  3.1 7.3 %all-to-all-start = ((s32[8,1,2]{2,1,0:T(1,128)}), s32[8,1,2]{2,1,0:T(1,128)S(1)}, u32[]{:S(2)}, u32[]{:S(2)}) async-start(s32[8,1,2]{2,1,0:T(1,128)} %copy.115), calls=%async_computation | async-start | bytes 8192 | tf_op jit(solution)/shard_map/all_to_all | solution.py:75
  13.6 10.6 %all-reduce = (f32[384]{0:T(512)S(1)}, f32[1536]{0:T(1024)S(1)}) all-reduce(f32[384]{0:T(512)S(1)} %fusion.39, f32[1536]{0:T(1024)S(1)} %fusion.36), channel_id=1, replica_groups=mesh['slab'=8,'head'=4] {'head'}, use_global_device_ids=true, to_apply=%region_1.0 | all-reduce | flops 1920 | bytes 15360 | tf_op jit(solution)/shard_map/psum | solution.py:39
  26.0 4.3 %reshape.332 = bf16[24,64,5,128]{3,2,1,0:T(8,128)(2,1)S(1)} reshape(bf16[1536,640]{1,0:T(8,128)(2,1)} %fusion.38) | data formatting | bytes 3932160 | tf_op jit(solution)/shard_map/reshape | solution.py:46
  35.8 5.7 %all-to-all-start.2 = ((bf16[8,2,64,128]{3,2,1,0:T(8,128)(2,1)}), bf16[8,2,64,128]{3,2,1,0:T(8,128)(2,1)S(1)}, u32[]{:S(2)}, u32[]{:S(2)}) async-start(bf16[8,2,64,128]{3,2,1,0:T(8,128)(2,1)} %bitcast.9), calls=%async_computation.2 | async-start | bytes 524288 | tf_op jit(solution)/shard_map/all_to_all | solution.py:80
  43.4 4.3 %reshape.328 = bf16[24,64,5,128]{3,2,1,0:T(8,128)(2,1)S(1)} reshape(bf16[1536,640]{1,0:T(8,128)(2,1)} %param.13) | data formatting | bytes 3932160 | tf_op jit(solution)/shard_map/reshape | solution.py:47
  52.4 6.1 %all-to-all-start.1 = ((bf16[8,2,64,128]{3,2,1,0:T(8,128)(2,1)}), bf16[8,2,64,128]{3,2,1,0:T(8,128)(2,1)}, u32[]{:S(2)}, u32[]{:S(2)}) async-start(bf16[8,2,64,128]{3,2,1,0:T(8,128)(2,1)} %bitcast.7), calls=%async_computation.1 | async-start | bytes 524288 | tf_op jit(solution)/shard_map/all_to_all | solution.py:81
  62.7 4.1 %all-to-all-done.1 = bf16[8,2,64,128]{3,2,1,0:T(8,128)(2,1)} async-done(((bf16[8,2,64,128]{3,2,1,0:T(8,128)(2,1)}), bf16[8,2,64,128]{3,2,1,0:T(8,128)(2,1)}, u32[]{:S(2)}, u32[]{:S(2)}) %all-to-all-start.1) | async-done | bytes 262176 | tf_op jit(solution)/shard_map/all_to_all | solution.py:81
  67.8 48.2 %while.32 = (s32[]{:T(128)}, bf16[3,2,64,5,128]{4,2,3,1,0:T(8,128)(2,1)}, f32[3,2,5,64,1]{3,2,1,4,0:T(8,128)}, s32[3,2,5,10]{3,1,2,0:T(2,128)}, bf16[24,64,5,128...) while((s32[]{:T(128)}, ...), condition=%wide.region_11.12_spmd.clone, body=%wide.region_8.11_spmd.clone.sunk | while | flops 257639456 | bytes 25921824 | solution.py:109
  77.0 4.0 %gather_fusion.1 = bf16[100,64,128]{2,1,0:T(8,128)(2,1)} fusion(bf16[24,64,5,128]{3,1,2,0:T(8,128)(2,1)} %get-tuple-element.587, s32[100]{0:T(128)S(1)} %reshape.553), kind=kCustom, calls=%fused_computation.clone.clone.1 | custom fusion | bytes 3277600 | tf_op jit(solution)/shard_map/while/body/eval_jaxpr/gather | solution.py:88
  93.1 4.0 %gather_fusion.1 = bf16[100,64,128]{2,1,0:T(8,128)(2,1)} fusion(bf16[24,64,5,128]{3,1,2,0:T(8,128)(2,1)} %get-tuple-element.587, s32[100]{0:T(128)S(1)} %reshape.553), kind=kCustom, calls=%fused_computation.clone.clone.1 | custom fusion | bytes 3277600 | tf_op jit(solution)/shard_map/while/body/eval_jaxpr/gather | solution.py:88
  109.1 4.0 %gather_fusion.1 = bf16[100,64,128]{2,1,0:T(8,128)(2,1)} fusion(bf16[24,64,5,128]{3,1,2,0:T(8,128)(2,1)} %get-tuple-element.587, s32[100]{0:T(128)S(1)} %reshape.553), kind=kCustom, calls=%fused_computation.clone.clone.1 | custom fusion | bytes 3277600 | tf_op jit(solution)/shard_map/while/body/eval_jaxpr/gather | solution.py:88
  123.3 211.4 %while.33 = (s32[]{:T(128)}, f32[24,64,5,128]{3,1,2,0:T(8,128)}, f32[24,64,5,128]{3,1,2,0:T(8,128)}, f32[16,64,128]{2,1,0:T(8,128)}, f32[16,64,128]{2,1,0:T(8,12...) while((s32[]{:T(128)}, f32[24,64,5,128]{3,1,2,0:T(8,128)}, ...), condition=%wide.region_18.19_spmd.clone, body=%wide.region_12.18_spmd.clone.sunk | while | flops 637420928 | bytes 79815728 | solution.py:148
  128.5 4.0 %gather_fusion.7 = bf16[100,64,128]{2,1,0:T(8,128)(2,1)} fusion(bf16[24,64,5,128]{3,1,2,0:T(8,128)(2,1)} %get-tuple-element.641, s32[100]{0:T(128)S(1)} %reshape.572), kind=kCustom, calls=%fused_computation.6.clone.clone.1 | custom fusion | bytes 3277600 | tf_op jit(solution)/shard_map/while/body/eval_jaxpr/gather | solution.py:88
  134.1 4.0 %gather_fusion.5 = bf16[100,64,128]{2,1,0:T(8,128)(2,1)} fusion(bf16[24,64,5,128]{3,1,2,0:T(8,128)(2,1)} %get-tuple-element.636, s32[100]{0:T(128)S(1)} %reshape.572), kind=kCustom, calls=%fused_computation.4.clone.clone.1 | custom fusion | bytes 3277600 | tf_op jit(solution)/shard_map/while/body/eval_jaxpr/gather | solution.py:88
  147.7 5.2 %scatter_fusion.2 = f32[16,64,128]{2,1,0:T(8,128)} fusion(f32[16,64,128]{2,1,0:T(8,128)} %get-tuple-element.614, s32[20]{0:T(128)S(1)} %reshape.571, f32[20,64,128]{2,1,0:T(8,128)} %bitcast.242), kind=kCustom, calls=%fused_computation.13.clone.clone.1 | custom fusion | flops 163840 | bytes 1966160 | tf_op jit(solution)/shard_map/while/body/eval_jaxpr/scatter-add | solution.py:142
  152.8 16.1 %scatter_fusion = f32[24,64,5,128]{3,1,2,0:T(8,128)} fusion(f32[24,64,5,128]{3,1,2,0:T(8,128)} %get-tuple-element.612, s32[100]{0:T(128)S(1)} %reshape.570, f32[100,64,128]{2,1,0:T(8,128)S(1)} %bitcast.233), kind=kCustom, calls=%fused_computation.11.clone.clone.1 | custom fusion | flops 819200 | bytes 9831200 | tf_op jit(solution)/shard_map/while/body/eval_jaxpr/scatter-add | solution.py:140
  172.3 5.2 %scatter_fusion.3 = f32[16,64,128]{2,1,0:T(8,128)} fusion(f32[16,64,128]{2,1,0:T(8,128)} %get-tuple-element.615, s32[20]{0:T(128)S(1)} %reshape.571, f32[20,64,128]{2,1,0:T(8,128)} %bitcast.241), kind=kCustom, calls=%fused_computation.14.clone.clone.1 | custom fusion | flops 163840 | bytes 1966160 | tf_op jit(solution)/shard_map/while/body/eval_jaxpr/scatter-add | solution.py:143
  177.5 16.2 %scatter_fusion.1 = f32[24,64,5,128]{3,1,2,0:T(8,128)} fusion(f32[24,64,5,128]{3,1,2,0:T(8,128)} %get-tuple-element.613, s32[100]{0:T(128)S(1)} %reshape.570, f32[100,64,128]{2,1,0:T(8,128)S(1)} %bitcast.232), kind=kCustom, calls=%fused_computation.12.clone.clone.1 | custom fusion | flops 819200 | bytes 9831200 | tf_op jit(solution)/shard_map/while/body/eval_jaxpr/scatter-add | solution.py:141
  198.9 4.0 %gather_fusion.7 = bf16[100,64,128]{2,1,0:T(8,128)(2,1)} fusion(bf16[24,64,5,128]{3,1,2,0:T(8,128)(2,1)} %get-tuple-element.641, s32[100]{0:T(128)S(1)} %reshape.572), kind=kCustom, calls=%fused_computation.6.clone.clone.1 | custom fusion | bytes 3277600 | tf_op jit(solution)/shard_map/while/body/eval_jaxpr/gather | solution.py:88
  204.5 4.0 %gather_fusion.5 = bf16[100,64,128]{2,1,0:T(8,128)(2,1)} fusion(bf16[24,64,5,128]{3,1,2,0:T(8,128)(2,1)} %get-tuple-element.636, s32[100]{0:T(128)S(1)} %reshape.572), kind=kCustom, calls=%fused_computation.4.clone.clone.1 | custom fusion | bytes 3277600 | tf_op jit(solution)/shard_map/while/body/eval_jaxpr/gather | solution.py:88
  218.1 5.2 %scatter_fusion.2 = f32[16,64,128]{2,1,0:T(8,128)} fusion(f32[16,64,128]{2,1,0:T(8,128)} %get-tuple-element.614, s32[20]{0:T(128)S(1)} %reshape.571, f32[20,64,128]{2,1,0:T(8,128)} %bitcast.242), kind=kCustom, calls=%fused_computation.13.clone.clone.1 | custom fusion | flops 163840 | bytes 1966160 | tf_op jit(solution)/shard_map/while/body/eval_jaxpr/scatter-add | solution.py:142
  223.3 16.2 %scatter_fusion = f32[24,64,5,128]{3,1,2,0:T(8,128)} fusion(f32[24,64,5,128]{3,1,2,0:T(8,128)} %get-tuple-element.612, s32[100]{0:T(128)S(1)} %reshape.570, f32[100,64,128]{2,1,0:T(8,128)S(1)} %bitcast.233), kind=kCustom, calls=%fused_computation.11.clone.clone.1 | custom fusion | flops 819200 | bytes 9831200 | tf_op jit(solution)/shard_map/while/body/eval_jaxpr/scatter-add | solution.py:140
  242.8 5.2 %scatter_fusion.3 = f32[16,64,128]{2,1,0:T(8,128)} fusion(f32[16,64,128]{2,1,0:T(8,128)} %get-tuple-element.615, s32[20]{0:T(128)S(1)} %reshape.571, f32[20,64,128]{2,1,0:T(8,128)} %bitcast.241), kind=kCustom, calls=%fused_computation.14.clone.clone.1 | custom fusion | flops 163840 | bytes 1966160 | tf_op jit(solution)/shard_map/while/body/eval_jaxpr/scatter-add | solution.py:143
  248.0 16.2 %scatter_fusion.1 = f32[24,64,5,128]{3,1,2,0:T(8,128)} fusion(f32[24,64,5,128]{3,1,2,0:T(8,128)} %get-tuple-element.613, s32[100]{0:T(128)S(1)} %reshape.570, f32[100,64,128]{2,1,0:T(8,128)S(1)} %bitcast.232), kind=kCustom, calls=%fused_computation.12.clone.clone.1 | custom fusion | flops 819200 | bytes 9831200 | tf_op jit(solution)/shard_map/while/body/eval_jaxpr/scatter-add | solution.py:141
  269.4 4.0 %gather_fusion.7 = bf16[100,64,128]{2,1,0:T(8,128)(2,1)} fusion(bf16[24,64,5,128]{3,1,2,0:T(8,128)(2,1)} %get-tuple-element.641, s32[100]{0:T(128)S(1)} %reshape.572), kind=kCustom, calls=%fused_computation.6.clone.clone.1 | custom fusion | bytes 3277600 | tf_op jit(solution)/shard_map/while/body/eval_jaxpr/gather | solution.py:88
  275.0 4.0 %gather_fusion.5 = bf16[100,64,128]{2,1,0:T(8,128)(2,1)} fusion(bf16[24,64,5,128]{3,1,2,0:T(8,128)(2,1)} %get-tuple-element.636, s32[100]{0:T(128)S(1)} %reshape.572), kind=kCustom, calls=%fused_computation.4.clone.clone.1 | custom fusion | bytes 3277600 | tf_op jit(solution)/shard_map/while/body/eval_jaxpr/gather | solution.py:88
  288.6 5.2 %scatter_fusion.2 = f32[16,64,128]{2,1,0:T(8,128)} fusion(f32[16,64,128]{2,1,0:T(8,128)} %get-tuple-element.614, s32[20]{0:T(128)S(1)} %reshape.571, f32[20,64,128]{2,1,0:T(8,128)} %bitcast.242), kind=kCustom, calls=%fused_computation.13.clone.clone.1 | custom fusion | flops 163840 | bytes 1966160 | tf_op jit(solution)/shard_map/while/body/eval_jaxpr/scatter-add | solution.py:142
  293.8 16.2 %scatter_fusion = f32[24,64,5,128]{3,1,2,0:T(8,128)} fusion(f32[24,64,5,128]{3,1,2,0:T(8,128)} %get-tuple-element.612, s32[100]{0:T(128)S(1)} %reshape.570, f32[100,64,128]{2,1,0:T(8,128)S(1)} %bitcast.233), kind=kCustom, calls=%fused_computation.11.clone.clone.1 | custom fusion | flops 819200 | bytes 9831200 | tf_op jit(solution)/shard_map/while/body/eval_jaxpr/scatter-add | solution.py:140
  313.3 5.2 %scatter_fusion.3 = f32[16,64,128]{2,1,0:T(8,128)} fusion(f32[16,64,128]{2,1,0:T(8,128)} %get-tuple-element.615, s32[20]{0:T(128)S(1)} %reshape.571, f32[20,64,128]{2,1,0:T(8,128)} %bitcast.241), kind=kCustom, calls=%fused_computation.14.clone.clone.1 | custom fusion | flops 163840 | bytes 1966160 | tf_op jit(solution)/shard_map/while/body/eval_jaxpr/scatter-add | solution.py:143
  318.5 16.2 %scatter_fusion.1 = f32[24,64,5,128]{3,1,2,0:T(8,128)} fusion(f32[24,64,5,128]{3,1,2,0:T(8,128)} %get-tuple-element.613, s32[100]{0:T(128)S(1)} %reshape.570, f32[100,64,128]{2,1,0:T(8,128)S(1)} %bitcast.232), kind=kCustom, calls=%fused_computation.12.clone.clone.1 | custom fusion | flops 819200 | bytes 9831200 | tf_op jit(solution)/shard_map/while/body/eval_jaxpr/scatter-add | solution.py:141
  334.7 16.2 %all_to_all.29 = f32[8,2,64,128]{3,2,1,0:T(8,128)S(1)} all-to-all(f32[8,2,64,128]{3,2,1,0:T(8,128)} %bitcast.245), channel_id=1, replica_groups=mesh['slab'=8,'head'=4] {'slab'}, dimensions={0} | all-to-all | bytes 1048576 | tf_op jit(solution)/shard_map/all_to_all | solution.py:155
  364.1 3.8 all-to-all-done.4
  (208 shorter events, 151.9 us)
Async XLA Ops:
  0.6 23.5 %copy-start.1 = (bf16[1536,640]{1,0:T(8,128)(2,1)S(1)}, bf16[1536,640]{1,0:T(8,128)(2,1)}, u32[]{:S(2)}) copy-start(bf16[1536,640]{1,0:T(8,128)(2,1)} %param.12) | copy-start | bytes 5898244
  0.6 23.5 %copy-start.4 = (f32[640]{0:T(1024)S(1)}, f32[640]{0:T(1024)}, u32[]{:S(2)}) copy-start(f32[640]{0:T(1024)} %param.15) | copy-start | bytes 7684
  3.1 29.1 %all-to-all-start = ((s32[8,1,2]{2,1,0:T(1,128)}), s32[8,1,2]{2,1,0:T(1,128)S(1)}, u32[]{:S(2)}, u32[]{:S(2)}) async-start(s32[8,1,2]{2,1,0:T(1,128)} %copy.115), calls=%async_computation | async-start | bytes 8192 | tf_op jit(solution)/shard_map/all_to_all | solution.py:75
  30.3 11.2 %copy-start.3 = (s32[6,5,12]{2,0,1:T(8,128)S(1)}, s32[6,5,12]{2,0,1:T(8,128)}, u32[]{:S(2)}) copy-start(s32[6,5,12]{2,0,1:T(8,128)} %param.17) | copy-start | bytes 4324
  35.8 16.6 %all-to-all-start.2 = ((bf16[8,2,64,128]{3,2,1,0:T(8,128)(2,1)}), bf16[8,2,64,128]{3,2,1,0:T(8,128)(2,1)S(1)}, u32[]{:S(2)}, u32[]{:S(2)}) async-start(bf16[8,2,64,128]{3,2,1,0:T(8,128)(2,1)} %bitcast.9), calls=%async_computation.2 | async-start | bytes 524288 | tf_op jit(solution)/shard_map/all_to_all | solution.py:80
  47.7 10.8 %copy-start.5 = (f32[640]{0:T(1024)S(1)}, f32[640]{0:T(1024)}, u32[]{:S(2)}) copy-start(f32[640]{0:T(1024)} %param.14) | copy-start | bytes 7684
  52.4 8.8 %copy-start.2 = (bf16[384,640]{1,0:T(8,128)(2,1)S(1)}, bf16[384,640]{1,0:T(8,128)(2,1)}, u32[]{:S(2)}) copy-start(bf16[384,640]{1,0:T(8,128)(2,1)} %param.16) | copy-start | bytes 1474564
  52.4 14.4 %all-to-all-start.1 = ((bf16[8,2,64,128]{3,2,1,0:T(8,128)(2,1)}), bf16[8,2,64,128]{3,2,1,0:T(8,128)(2,1)}, u32[]{:S(2)}, u32[]{:S(2)}) async-start(bf16[8,2,64,128]{3,2,1,0:T(8,128)(2,1)} %bitcast.7), calls=%async_computation.1 | async-start | bytes 524288 | tf_op jit(solution)/shard_map/all_to_all | solution.py:81
  141.5 1.9 copy-start
  211.9 1.9 copy-start
  282.4 1.9 copy-start
  334.7 19.9 %copy-start.6 = (s32[8,2,1]{0,1,2:T(2,128)S(1)}, s32[8,2,1]{0,1,2:T(2,128)}, u32[]{:S(2)}) copy-start(s32[8,2,1]{0,1,2:T(2,128)} %get-tuple-element.380) | copy-start | bytes 196
  350.9 17.0 %all-to-all-start.4 = ((f32[8,2,64,128]{3,2,1,0:T(8,128)}), f32[8,2,64,128]{3,2,1,0:T(8,128)S(1)}, u32[]{:S(2)}, u32[]{:S(2)}) async-start(f32[8,2,64,128]{3,2,1,0:T(8,128)} %bitcast.244), calls=%async_computation.4 | async-start | bytes 1048576 | tf_op jit(solution)/shard_map/all_to_all | solution.py:162
where the time goes:
time: 387 us; the launch traced here: 380 us
  other arithmetic  173 us (45%)
  local copies, waits for them, and re-layouts  113 us (29%)
  matrix products  34.6 us (9%)
  blocking collectives  26.8 us (7%)
  starting transfers between devices  22.8 us (6%)
  waiting for transfers between devices  7.9 us (2%)
    scatter-add x3, other arithmetic, backward_block(): value_grad.at[near_block, :, head_ids, :].add(grad_values[:, :, :NEAR])  48.6 us
    scatter-add x3, other arithmetic, backward_block(): key_grad.at[near_block, :, head_ids, :].add(grad_keys[:, :, :NEAR])  48.5 us
    gather x12, local copies, waits for them, and re-layouts, gather_kept(): source_table[near_block, :, head_ids, :]  44.5 us
    all_to_all x1, blocking collectives, local(): lax.all_to_all(far_key_grad.reshape(slab_count, CAP, TILE, head_size), 's...  16.2 us
    scatter-add x3, other arithmetic, backward_block(): far_value_grad = far_value_grad.at[use_block].add(grad_values[:, :, NEAR:])  15.6 us
    scatter-add x3, other arithmetic, backward_block(): far_key_grad = far_key_grad.at[use_block].add(grad_keys[:, :, NEAR:])  15.5 us
    concatenate x12, other arithmetic, gather_kept(): jnp.concatenate((source_table[near_block, :, head_ids, :], fetched_pool[u...  14.9 us
    gather x12, local copies, waits for them, and re-layouts, gather_kept(): fetched_pool[use_block]  13 us
  transfers between devices with their start and end apart: 4, of which 2 were waited for; matrix products, arithmetic and copies ran while one was open for 9% of the time, Pallas kernels for 0%

commit v1 on v0

v1 whole, which is shorter than its diff:
```python
import functools
import math

import jax
import jax.numpy as jnp
from jax import lax
from jax.experimental import pallas as pl
from jax.experimental.pallas import tpu as pltpu
from jax.sharding import PartitionSpec as P

TILE = 64
NEAR = 10
CAP = 2
HD = 128

NORM_EPSILON = 1e-06
MASKED = -1e30

VMEM = pl.BlockSpec(memory_space=pltpu.VMEM)
SMEM = pl.BlockSpec(memory_space=pltpu.SMEM)
ANY = pl.BlockSpec(memory_space=pl.ANY)
NT = (((1,), (1,)), ((), ()))
NN = (((1,), (0,)), ((), ()))
LOG2E = math.log2(math.e)


def dot(a, b, dims):
    return lax.dot_general(a, b, dims, preferred_element_type=jnp.float32)


def each(count, body):
    if count <= 16:
        for i in range(count):
            body(i)
    else:
        lax.fori_loop(0, count, lambda i, c: (body(i), c)[1], 0)


def inverse_rms(part_refs, full_width):
    total = part_refs[0][...]
    for ref in part_refs[1:]:
        total = total + ref[...]
    return lax.rsqrt(total / full_width + NORM_EPSILON).T


def pair_of(code, head_step):
    return code // head_step, code % head_step


def gather_kernel(
    full_width, head_step, parts, wanted, *refs
):
    part_refs, (gain, k_raw, values, out, k_buf, scale, sems) = refs[:parts], refs[parts:]
    slots = out.shape[0] * CAP

    def copies(s):
        tile, head = pair_of(wanted[s // CAP, s % CAP], head_step)
        rows = pl.ds(pl.multiple_of(tile * TILE, TILE), TILE)
        cols = pl.ds(pl.multiple_of(head * HD, HD), HD)
        return (
            pltpu.make_async_copy(k_raw.at[rows, cols], k_buf.at[s], sems.at[0, s]),
            pltpu.make_async_copy(
                values.at[rows, cols], out.at[s // CAP, CAP + s % CAP], sems.at[1, s]
            ),
        )

    each(slots, lambda s: [c.start() for c in copies(s)])
    inverse = inverse_rms(part_refs, full_width)
    for j in range(scale.shape[0] // HD):
        scale[j * HD : (j + 1) * HD, :] = jnp.broadcast_to(inverse[:, j : j + 1], (HD, HD))

    def normalize(s):
        for c in copies(s):
            c.wait()
        tile, head = pair_of(wanted[s // CAP, s % CAP], head_step)
        rows = pl.ds(pl.multiple_of(tile * TILE, TILE), TILE)
        out[s // CAP, s % CAP] = (
            k_buf[s].astype(jnp.float32) * scale[rows, :] * gain[pl.ds(head, 1), :]
        ).astype(jnp.bfloat16)

    each(slots, normalize)


def attend_kernel(full_width, head_step, parts, wanted, use_slot, *refs):
    part_refs = refs[:parts]
    (q_raw, k_raw, values, cot, q_gain, k_gain, mask, far,
     attn, dq, dk, dv, far_grad, kept_k, kept_v,
     kn, qn, s_scr, p_scr, ds_scr, fk_acc, fv_acc) = refs[parts:]
    head = pl.program_id(0)
    key_tokens = k_raw.shape[0]
    query_tokens = q_raw.shape[0]
    key_tiles = key_tokens // TILE
    pairs = query_tokens // HD
    score_scale = 1.0 / math.sqrt(HD)
    slots = far.shape[0] * CAP

    inverse = inverse_rms(part_refs, full_width)
    for j in range(key_tokens // HD):
        rows = slice(j * HD, (j + 1) * HD)
        kn[rows, :] = (
            k_raw[rows, :].astype(jnp.float32) * inverse[:, j : j + 1] * k_gain[0]
        ).astype(jnp.bfloat16)
    first = key_tokens // HD
    for j in range(pairs):
        rows = slice(j * HD, (j + 1) * HD)
        qn[rows, :] = (
            q_raw[rows, :].astype(jnp.float32) * inverse[:, first + j : first + j + 1] * q_gain[0]
        ).astype(jnp.bfloat16)

    @pl.when(head == 0)
    def _():
        fk_acc[...] = jnp.zeros_like(fk_acc)
        fv_acc[...] = jnp.zeros_like(fv_acc)

    left = lax.broadcasted_iota(jnp.int32, (2 * TILE, HD), 1) < TILE
    exponent = score_scale * LOG2E

    def far_tiles(p, kind):
        tiles = []
        for i in (2 * p, 2 * p + 1):
            for f in range(CAP):
                s = use_slot[i, head * CAP + f]
                tiles.append(far[s // CAP, kind * CAP + s % CAP])
        return jnp.concatenate(tiles, axis=0)

    def pick(x):
        return jnp.where(left, x[: 2 * TILE], x[2 * TILE :])

    def spread(x):
        zero = jnp.zeros_like(x)
        return jnp.concatenate((jnp.where(left, x, zero), jnp.where(left, zero, x)), axis=0)

    top = None
    for t in range(key_tiles):
        rows = slice(t * TILE, (t + 1) * TILE)
        block = dot(kn[rows, :], qn[...], NT) * exponent + mask[0, t : t + 1, :]
        s_scr[rows, :] = block
        block = jnp.max(block, axis=0, keepdims=True)
        top = block if top is None else jnp.maximum(top, block)

    for p in range(pairs):
        cols = slice(p * HD, (p + 1) * HD)
        q_p = qn[cols, :]
        c_p = cot[cols, :]
        far_k = far_tiles(p, 0)
        far_v = far_tiles(p, 1)
        far_s = pick(dot(far_k, q_p, NT)) * exponent
        peak = jnp.maximum(top[:, cols], jnp.max(far_s, axis=0, keepdims=True))
        far_e = jnp.exp2(far_s - peak)
        total = jnp.sum(far_e, axis=0, keepdims=True)
        for t in range(key_tiles):
            rows = slice(t * TILE, (t + 1) * TILE)
            e = jnp.exp2(s_scr[rows, cols] - peak)
            s_scr[rows, cols] = e
            total = total + jnp.sum(e, axis=0, keepdims=True)
        norm = 1.0 / total
        for t in range(key_tiles):
            rows = slice(t * TILE, (t + 1) * TILE)
            p_scr[rows, cols] = (s_scr[rows, cols] * norm).astype(jnp.bfloat16)
        far_p = (far_e * norm).astype(jnp.bfloat16)
        far_p4 = spread(far_p)
        out_t = dot(values[...].T, p_scr[:, cols], NN) + dot(far_v.T, far_p4, NN)
        out_b = out_t.astype(jnp.bfloat16)
        attn[cols, :] = out_b.T
        delta = jnp.sum(
            c_p.T.astype(jnp.float32) * out_b.astype(jnp.float32), axis=0, keepdims=True
        )
        far_dp = pick(dot(far_v, c_p, NT))
        far_ds = (far_p.astype(jnp.float32) * (far_dp - delta) * score_scale).astype(jnp.bfloat16)
        far_ds4 = spread(far_ds)
        grad_k = dot(far_ds4, q_p, NN)
        grad_v = dot(far_p4, c_p, NN)
        b = 0
        for i in (2 * p, 2 * p + 1):
            for f in range(CAP):
                s = use_slot[i, head * CAP + f]
                fk_acc[s] += grad_k[b * TILE : (b + 1) * TILE]
                fv_acc[s] += grad_v[b * TILE : (b + 1) * TILE]
                b += 1
        for t in range(key_tiles):
            rows = slice(t * TILE, (t + 1) * TILE)
            dp = dot(values[rows, :], c_p, NT)
            ds_scr[rows, cols] = (
                p_scr[rows, cols].astype(jnp.float32) * (dp - delta) * score_scale
            ).astype(jnp.bfloat16)
        dq_t = dot(kn[...].T, ds_scr[:, cols], NN) + dot(far_k.T, far_ds4, NN)
        dq[cols, :] = dq_t.astype(jnp.bfloat16).T

    grad_k = dot(ds_scr[...], qn[...], NN)
    grad_v = dot(p_scr[...], cot[...], NN)
    dk[...] = grad_k.astype(jnp.bfloat16)
    dv[...] = grad_v.astype(jnp.bfloat16)
    s_scr[:, :HD] = grad_k
    s_scr[:, HD : 2 * HD] = grad_v

    def keep(s):
        tile, owner = pair_of(wanted[s // CAP, s % CAP], head_step)

        @pl.when(owner == head)
        def _():
            rows = pl.ds(pl.multiple_of(tile * TILE, TILE), TILE)
            kept_k[s] = s_scr[rows, :HD]
            kept_v[s] = s_scr[rows, HD : 2 * HD]

    each(slots, keep)

    @pl.when(head == pl.num_programs(0) - 1)
    def _():
        def send(s):
            far_grad[s // CAP, s % CAP] = fk_acc[s].astype(jnp.bfloat16)
            far_grad[s // CAP, CAP + s % CAP] = fv_acc[s].astype(jnp.bfloat16)

        each(slots, send)


def finish_kernel(head_step, wanted, back, kept_k, kept_v, dk_in, dv_in, dk, dv,
                  acc_k, acc_v, out_k, out_v, sems):
    del dk_in, dv_in
    slots = back.shape[0] * CAP
    acc_k[...] = kept_k[...]
    acc_v[...] = kept_v[...]

    def add(s):
        code = wanted[s // CAP, s % CAP]

        def earlier(r, found):
            r = s - 1 - r
            return jnp.where(wanted[r // CAP, r % CAP] == code, r, found)

        slot = s
        if isinstance(s, int):
            for r in range(s):
                slot = earlier(r, slot)
        else:
            slot = lax.fori_loop(0, s, earlier, s)
        acc_k[slot] += back[s // CAP, s % CAP].astype(jnp.float32)
        acc_v[slot] += back[s // CAP, CAP + s % CAP].astype(jnp.float32)
        return slot

    def copies(s):
        tile, head = pair_of(wanted[s // CAP, s % CAP], head_step)
        rows = pl.ds(pl.multiple_of(tile * TILE, TILE), TILE)
        cols = pl.ds(pl.multiple_of(head * HD, HD), HD)
        return (
            pltpu.make_async_copy(out_k.at[s], dk.at[rows, cols], sems.at[0, s]),
            pltpu.make_async_copy(out_v.at[s], dv.at[rows, cols], sems.at[1, s]),
        )

    def first_of(s):
        code = wanted[s // CAP, s % CAP]

        def earlier(r, found):
            return jnp.where(wanted[r // CAP, r % CAP] == code, True, found)

        found = jnp.bool_(False)
        if isinstance(s, int):
            for r in range(s):
                found = earlier(r, found)
        else:
            found = lax.fori_loop(0, s, earlier, found)
        return jnp.logical_not(found)

    each(slots, add)
    out_k[...] = acc_k[...].astype(jnp.bfloat16)
    out_v[...] = acc_v[...].astype(jnp.bfloat16)

    def start(s):
        @pl.when(first_of(s))
        def _():
            for c in copies(s):
                c.start()

    def finish(s):
        @pl.when(first_of(s))
        def _():
            for c in copies(s):
                c.wait()

    each(slots, start)
    each(slots, finish)


def local(q_raw, k_raw, values, q_gain, k_gain, cotangent, kept_tiles):
    slab_count = lax.axis_size("slab")
    group_count = lax.axis_size("head")
    own_slab = lax.axis_index("slab")
    query_tiles, head_count, kept_count = kept_tiles.shape
    local_width = q_raw.shape[1]
    key_tiles = k_raw.shape[0] // TILE
    query_tokens, key_tokens = q_raw.shape[0], k_raw.shape[0]
    full_width = local_width * group_count
    head_step = pl.next_power_of_2(head_count)
    slots = slab_count * CAP
    vmem = pltpu.CompilerParams(vmem_limit_bytes=56 << 20)

    head_ids = jnp.arange(head_count, dtype=jnp.int32)[None, :, None]
    far_global = kept_tiles[:, :, NEAR:]
    far_owner = far_global // key_tiles
    code = far_global % key_tiles * head_step + head_ids
    slab_ids = jnp.arange(slab_count, dtype=jnp.int32)
    mine = far_owner.reshape(1, -1) == slab_ids[:, None]
    flat = code.reshape(1, -1)
    low = jnp.min(jnp.where(mine, flat, 1 << 20), axis=1)
    high = jnp.max(jnp.where(mine, flat, 0), axis=1)
    low = jnp.where(low == 1 << 20, 0, low)
    lane = jnp.arange(HD, dtype=jnp.int32)[None, :]
    request = jnp.where(lane == 0, low[:, None], high[:, None])
    wanted = lax.all_to_all(request, "slab", split_axis=0, concat_axis=0, tiled=True)
    use_slot = far_owner * CAP + (code != low[far_owner]).astype(jnp.int32)
    use_slot = use_slot.reshape(query_tiles, head_count * (kept_count - NEAR))

    k_sum = jnp.sum(jnp.square(k_raw.astype(jnp.float32)), axis=1)
    q_sum = jnp.sum(jnp.square(q_raw.astype(jnp.float32)), axis=1)
    stat_rows = -(-(key_tokens + query_tokens) // (8 * HD)) * 8
    pad = stat_rows * HD - key_tokens - query_tokens
    stats = jnp.concatenate((k_sum, q_sum, jnp.zeros((pad,), jnp.float32))).reshape(stat_rows, HD)
    parts = [stats]
    for step in range(1, group_count):
        parts.append(
            lax.ppermute(
                stats, "head", [(i, (i + step) % group_count) for i in range(group_count)]
            )
        )

    outgoing = pl.pallas_call(
        functools.partial(gather_kernel, full_width, head_step, group_count),
        out_shape=jax.ShapeDtypeStruct((slab_count, 2 * CAP, TILE, HD), jnp.bfloat16),
        in_specs=[SMEM] + [VMEM] * group_count + [VMEM, ANY, ANY],
        out_specs=VMEM,
        scratch_shapes=[
            pltpu.VMEM((slots, TILE, HD), jnp.bfloat16),
            pltpu.VMEM((key_tokens, HD), jnp.float32),
            pltpu.SemaphoreType.DMA((2, slots)),
        ],
        compiler_params=vmem,
        name="gather_far",
    )(wanted, *parts, k_gain.reshape(head_count, HD), k_raw, values)
    far = lax.all_to_all(outgoing, "slab", split_axis=0, concat_axis=0, tiled=True)

    near = kept_tiles[:, :, :NEAR] - own_slab * key_tiles
    tile_ids = jnp.arange(key_tiles, dtype=jnp.int32)
    kept = jnp.any(near[:, :, :, None] == tile_ids, axis=2)
    mask = jnp.where(kept, 0.0, MASKED).astype(jnp.float32).transpose(1, 2, 0)
    mask = jnp.repeat(mask, TILE, axis=2)

    def column(tokens):
        return pl.BlockSpec((tokens, HD), lambda h, *_: (0, h))

    def whole(*shape):
        return pl.BlockSpec(shape, lambda h, *_: (0,) * len(shape))

    gain_spec = pl.BlockSpec((1, 1, HD), lambda h, *_: (h, 0, 0))
    attn_out, dq_normed, dk, dv, far_grad, kept_k, kept_v = pl.pallas_call(
        functools.partial(attend_kernel, full_width, head_step, group_count),
        grid_spec=pltpu.PrefetchScalarGridSpec(
            num_scalar_prefetch=2,
            grid=(head_count,),
            in_specs=[whole(stat_rows, HD)] * group_count
            + [
                column(query_tokens),
                column(key_tokens),
                column(key_tokens),
                column(query_tokens),
                gain_spec,
                gain_spec,
                pl.BlockSpec((1, key_tiles, query_tokens), lambda h, *_: (h, 0, 0)),
                whole(slab_count, 2 * CAP, TILE, HD),
            ],
            out_specs=[
                column(query_tokens),
                column(query_tokens),
                column(key_tokens),
                column(key_tokens),
                whole(slab_count, 2 * CAP, TILE, HD),
                whole(slots, TILE, HD),
                whole(slots, TILE, HD),
            ],
            scratch_shapes=[
                pltpu.VMEM((key_tokens, HD), jnp.bfloat16),
                pltpu.VMEM((query_tokens, HD), jnp.bfloat16),
                pltpu.VMEM((key_tokens, query_tokens), jnp.float32),
                pltpu.VMEM((key_tokens, query_tokens), jnp.bfloat16),
                pltpu.VMEM((key_tokens, query_tokens), jnp.bfloat16),
                pltpu.VMEM((slots, TILE, HD), jnp.float32),
                pltpu.VMEM((slots, TILE, HD), jnp.float32),
            ],
        ),
        out_shape=[
            jax.ShapeDtypeStruct((query_tokens, local_width), jnp.bfloat16),
            jax.ShapeDtypeStruct((query_tokens, local_width), jnp.bfloat16),
            jax.ShapeDtypeStruct((key_tokens, local_width), jnp.bfloat16),
            jax.ShapeDtypeStruct((key_tokens, local_width), jnp.bfloat16),
            jax.ShapeDtypeStruct((slab_count, 2 * CAP, TILE, HD), jnp.bfloat16),
            jax.ShapeDtypeStruct((slots, TILE, HD), jnp.float32),
            jax.ShapeDtypeStruct((slots, TILE, HD), jnp.float32),
        ],
        compiler_params=vmem,
        name="attend",
    )(
        wanted, use_slot, *parts, q_raw, k_raw, values, cotangent,
        q_gain.reshape(head_count, 1, HD), k_gain.reshape(head_count, 1, HD), mask, far,
    )

    back = lax.all_to_all(far_grad, "slab", split_axis=0, concat_axis=0, tiled=True)
    dk, dv = pl.pallas_call(
        functools.partial(finish_kernel, head_step),
        out_shape=[jax.ShapeDtypeStruct((key_tokens, local_width), jnp.bfloat16)] * 2,
        in_specs=[SMEM, VMEM, VMEM, VMEM, ANY, ANY],
        out_specs=[ANY, ANY],
        scratch_shapes=[
            pltpu.VMEM((slots, TILE, HD), jnp.float32),
            pltpu.VMEM((slots, TILE, HD), jnp.float32),
            pltpu.VMEM((slots, TILE, HD), jnp.bfloat16),
            pltpu.VMEM((slots, TILE, HD), jnp.bfloat16),
            pltpu.SemaphoreType.DMA((2, slots)),
        ],
        input_output_aliases={4: 0, 5: 1},
        compiler_params=vmem,
        name="finish",
    )(wanted, back, kept_k, kept_v, dk, dv)
    return attn_out, dq_normed, dk, dv


def solution(mesh):
    tokens = P("slab", "head")
    return jax.shard_map(
        local,
        mesh=mesh,
        in_specs=(tokens, tokens, tokens, P("head"), P("head"), tokens, P("slab", "head", None)),
        out_specs=(tokens, tokens, tokens, tokens),
        check_vma=False,
    )
```

time: 387 us -> 101 us (0.26); the launches traced: 380 us -> 99.9 us
  other arithmetic: 173 us -> 4.28 us
  local copies, waits for them, and re-layouts: 113 us -> 5.74 us
  Pallas kernels: 0 us -> 41.3 us
  matrix products: 34.6 us -> 0 us
  starting transfers between devices: 22.8 us -> 12.6 us
  waiting for transfers between devices: 7.9 us -> 16.8 us
  blocking collectives: 26.8 us -> 18.4 us
    scatter-add x14 -> x0, other arithmetic: 134 us -> none  [the longest x3 48.6 us: backward_block(): value_grad.at[near_block, :, head_ids, :].add(grad_values[:, :, :NEAR])]
    gather x28 -> x2, local copies, waits for them, and re-layouts: 64.1 us -> 0.87 us  [local(): use_slot = far_owner * CAP + (code != low[far_owner]).astype(jnp.int32)]
    pallas_call x0 -> x3, Pallas kernels: none -> 41.3 us  [the longest x1 35.5 us: local(): pl.pallas_call(functools.partial(attend_kernel, full_width, head_step, gr...]
    dot_general x21 -> x0, matrix products: 34.6 us -> none  [the longest x6 10.6 us: tile_scores(): jnp.einsum('jqhd,jhkd->jhqk', queries, kept_keys, preferred_element_type=...]
    concatenate x29 -> x0, other arithmetic: 20.2 us -> none  [the longest x12 14.9 us: gather_kept(): jnp.concatenate((source_table[near_block, :, head_ids, :], fetched_pool[u...]
    all_to_all x3 -> x1, starting transfers between devices: 15.5 us -> 3.51 us  [local(): lax.all_to_all(outgoing, 'slab', split_axis=0, concat_axis=0, tiled=True)]
    psum x1 -> x0, blocking collectives: 10.6 us -> none  [local(): q_sum, k_sum = lax.psum((q_sum, k_sum), 'head')]
    reshape x6 -> x4, local copies, waits for them, and re-layouts: 12.9 us -> 2.7 us  [the longest x1 0.84 us: local(): mask = jnp.repeat(mask, TILE, axis=2)]
  transfers between devices with their start and end apart: 4 -> 5, of which waited for: 2 -> 2; matrix products, arithmetic and copies ran while one was open for 9% -> 5% of each run, Pallas kernels for 0% -> 0%
where the time goes in v1:
time: 101 us; the launch traced here: 99.9 us
  Pallas kernels  41.3 us (41%)
  blocking collectives  18.4 us (18%)
  waiting for transfers between devices  16.8 us (17%)
  starting transfers between devices  12.6 us (12%)
  local copies, waits for them, and re-layouts  5.74 us (6%)
  other arithmetic  4.28 us (4%)
    pallas_call x1, Pallas kernels, local(): pl.pallas_call(functools.partial(attend_kernel, full_width, head_step, gr...  35.5 us
    all_to_all x1, blocking collectives, local(): lax.all_to_all(far_grad, 'slab', split_axis=0, concat_axis=0, tiled=True)  18.4 us
    all_to_all x1, waiting for transfers between devices, local(): lax.all_to_all(outgoing, 'slab', split_axis=0, concat_axis=0, tiled=True)  11.7 us
    all_to_all x1, starting transfers between devices, local(): lax.all_to_all(request, 'slab', split_axis=0, concat_axis=0, tiled=True)  5.84 us
    all_to_all x1, waiting for transfers between devices, local(): lax.all_to_all(request, 'slab', split_axis=0, concat_axis=0, tiled=True)  5.18 us
    all_to_all x1, starting transfers between devices, local(): lax.all_to_all(outgoing, 'slab', split_axis=0, concat_axis=0, tiled=True)  3.51 us
    ppermute x3, starting transfers between devices, local(): lax.ppermute(stats, 'head', [(i, (i + step) % group_count) for i in range...  3.23 us
    pallas_call x1, Pallas kernels, local(): pl.pallas_call(functools.partial(gather_kernel, full_width, head_step, gr...  3.03 us
  transfers between devices with their start and end apart: 5, of which 2 were waited for; matrix products, arithmetic and copies ran while one was open for 5% of the time, Pallas kernels for 0%

profile of v1, /device:TPU:0, one launch (start us, length us, event | category | flops | bytes accessed | tf_op | source)
XLA Modules:
  0.0 99.9 jit_solution(4203985774147415999)
XLA Ops:
  0.7 1.2 %multiply_reduce_fusion.1 = f32[384]{0:T(512)S(1)} fusion(bf16[384,640]{1,0:T(8,128)(2,1)} %refs_4_.1), kind=kLoop, calls=%fused_computation.2 | loop fusion | flops 736896 | bytes 493056 | tf_op jit(solution)/shard_map/reduce_sum | solution.py:313
  1.9 2.0 %multiply_reduce_fusion = f32[1536]{0:T(1024)S(1)} fusion(bf16[1536,640]{1,0:T(8,128)(2,1)} %refs_5_.3), kind=kLoop, calls=%fused_computation.1 | loop fusion | flops 2947584 | bytes 1972224 | tf_op jit(solution)/shard_map/reduce_sum | solution.py:312
  3.9 2.4 %collective-permute-start.2 = (f32[16,128]{1,0:T(8,128)S(1)}, f32[16,128]{1,0:T(8,128)S(1)}, u32[]{:S(2)}, u32[]{:S(2)}) collective-permute-start(f32[16,128]{1,0:T(8,128)S(1)} %maximum_bitcast_fusion.refs_0_), channel_id=1, source_target_pairs={{0,3},{1,0},{2,1},{3,2},{4,7},{5,4},{6,5},{7,6},{8,11},{9,8},{10,9... | collective-permute-start | bytes 24584 | tf_op jit(solution)/shard_map/ppermute | solution.py:320
  6.3 0.6 collective-permute-start.1
  7.0 0.2 collective-permute-start
  7.2 0.1 slice.6
  7.3 0.1 broadcast_in_dim.73
  7.4 0.1 eq.50
  7.5 0.2 select_reduce_fusion.1
  7.7 0.7 broadcast_select_fusion
  8.3 5.8 %all-to-all-start = ((s32[8,1,128]{2,1,0:T(1,128)}), s32[8,1,128]{2,1,0:T(1,128)S(1)}, u32[]{:S(2)}, u32[]{:S(2)}) async-start(s32[8,1,128]{2,1,0:T(1,128)} %broadcast_select_fusion), calls=%async_computation | async-start | bytes 8192 | tf_op jit(solution)/shard_map/all_to_all | solution.py:308
  14.2 0.6 reshape.101.refs_8_
  14.8 0.6 reshape.102.refs_9_
  15.4 5.2 %all-to-all-done = s32[8,1,128]{2,1,0:T(1,128)S(1)} async-done(((s32[8,1,128]{2,1,0:T(1,128)}), s32[8,1,128]{2,1,0:T(1,128)S(1)}, u32[]{:S(2)}, u32[]{:S(2)}) %all-to-all-start) | async-done | bytes 4128 | tf_op jit(solution)/shard_map/all_to_all | solution.py:308
  20.6 0.5 copy-done.3
  21.1 0.0 copy-done.4
  21.2 3.0 %gather_far.1 = bf16[8,4,64,128]{3,2,1,0:T(8,128)(2,1)} custom-call(s32[8,128]{1,0:T(8,128)} %bitcast.6, f32[16,128]{1,0:T(8,128)} %copy-done.2, f32[16,128]{1,0:T(8,128)} %copy-done.6, f32[16,128]{1,0:T(8,128)} %copy-done.5, f32[16,128]{1,0:T(8,128)} %copy-done.4, f32[5,128]{1,0:T(8,128)} %bitcast.9, bf16[1536,640]{1,0:T(8,128)(2,1)} %refs_5_.3, ...), custom_call_target="tpu_custom_call" | custom-call | tf_op jit(solution)/shard_map/gather_far/pallas_call | solution.py:325
  24.2 3.5 %all-to-all-start.1 = ((bf16[8,4,64,128]{3,2,1,0:T(8,128)(2,1)}), bf16[8,4,64,128]{3,2,1,0:T(8,128)(2,1)S(1)}, u32[]{:S(2)}, u32[]{:S(2)}) async-start(bf16[8,4,64,128]{3,2,1,0:T(8,128)(2,1)} %gather_far.1), calls=%async_computation.1 | async-start | bytes 1048576 | tf_op jit(solution)/shard_map/all_to_all | solution.py:338
  27.7 0.1 copy.27
  27.9 0.1 fusion
  28.0 0.1 copy.28
  28.1 0.1 reshape.107
  28.2 0.8 gather_fusion
  29.0 0.1 reshape.106
  29.1 0.7 reshape.115.use_slot
  29.8 0.2 broadcast_in_dim.84
  30.0 0.8 reshape.103.refs_10_
  30.8 11.7 %all-to-all-done.1.refs_11_ = bf16[8,4,64,128]{3,2,1,0:T(8,128)(2,1)S(1)} async-done(((bf16[8,4,64,128]{3,2,1,0:T(8,128)(2,1)}), bf16[8,4,64,128]{3,2,1,0:T(8,128)(2,1)S(1)}, u32[]{:S(2)}, u32[]{:S(2)}) %all-to-all-start.1) | async-done | bytes 524320 | tf_op jit(solution)/shard_map/all_to_all | solution.py:338
  42.5 0.8 copy-done
  43.3 35.5 %attend.1 = (bf16[384,640]{1,0:T(8,128)(2,1)}, bf16[384,640]{1,0:T(8,128)(2,1)}, bf16[1536,640]{1,0:T(8,128)(2,1)}, bf16[1536,640]{1,0:T(8,128)(2,1)}, bf16[8,4,...) custom-call(s32[8,128]{1,0:T(8,128)} %bitcast.7, s32[6,10]{1,0:T(8,128)} %reshape.115.use_slot, ...), custom_call_target="tpu_custom_call" | custom-call | tf_op jit(solution)/shard_map/attend/pallas_call | solution.py:353
  78.8 18.4 %all_to_all.18.back = bf16[8,4,64,128]{3,2,1,0:T(8,128)(2,1)} all-to-all(bf16[8,4,64,128]{3,2,1,0:T(8,128)(2,1)} %get-tuple-element.15), channel_id=1, replica_groups=mesh['slab'=8,'head'=4] {'slab'}, dimensions={0} | all-to-all | bytes 1048576 | tf_op jit(solution)/shard_map/all_to_all | solution.py:404
  97.2 2.7 %finish.1 = (bf16[1536,640]{1,0:T(8,128)(2,1)}, bf16[1536,640]{1,0:T(8,128)(2,1)}) custom-call(s32[8,128]{1,0:T(8,128)} %bitcast.8, bf16[8,4,64,128]{3,2,1,0:T(8,128)(2,1)} %all_to_all.18.back, f32[16,64,128]{2,1,0:T(8,128)} %get-tuple-element.16.kept_k, f32[16,64,128]{2,1,0:T(8,128)} %get-tuple-element.17.kept_v, ...), custom_call_target="tpu_custom_call", output_to_operand_aliasing={{0}: (4, {}), {1}: (5, {})} | custom-call | tf_op jit(solution)/shard_map/finish/pallas_call | solution.py:405
  (27 shorter events, 0.2 us)
Async XLA Ops:
  0.6 6.5 %copy-start.1 = (s32[6,5,12]{2,0,1:T(8,128)S(1)}, s32[6,5,12]{2,0,1:T(8,128)}, u32[]{:S(2)}) copy-start(s32[6,5,12]{2,0,1:T(8,128)} %param.13) | copy-start | bytes 4324
  0.6 13.5 %copy-start.8 = (f32[640]{0:T(1024)S(1)}, f32[640]{0:T(1024)}, u32[]{:S(2)}) copy-start(f32[640]{0:T(1024)} %param.10) | copy-start | bytes 7684
  0.7 14.1 %copy-start.7 = (f32[640]{0:T(1024)S(1)}, f32[640]{0:T(1024)}, u32[]{:S(2)}) copy-start(f32[640]{0:T(1024)} %param.11) | copy-start | bytes 7684
  3.9 16.7 %copy-start.2 = (f32[16,128]{1,0:T(8,128)}, f32[16,128]{1,0:T(8,128)S(1)}, u32[]{:S(2)}) copy-start(f32[16,128]{1,0:T(8,128)S(1)} %maximum_bitcast_fusion.refs_0_) | copy-start | bytes 24580
  3.9 16.6 %collective-permute-start.2 = (f32[16,128]{1,0:T(8,128)S(1)}, f32[16,128]{1,0:T(8,128)S(1)}, u32[]{:S(2)}, u32[]{:S(2)}) collective-permute-start(f32[16,128]{1,0:T(8,128)S(1)} %maximum_bitcast_fusion.refs_0_), channel_id=1, source_target_pairs={{0,3},{1,0},{2,1},{3,2},{4,7},{5,4},{6,5},{7,6},{8,11},{9,8},{10,9... | collective-permute-start | bytes 24584 | tf_op jit(solution)/shard_map/ppermute | solution.py:320
  6.3 14.2 %collective-permute-start.1 = (f32[16,128]{1,0:T(8,128)S(1)}, f32[16,128]{1,0:T(8,128)S(1)}, u32[]{:S(2)}, u32[]{:S(2)}) collective-permute-start(f32[16,128]{1,0:T(8,128)S(1)} %maximum_bitcast_fusion.refs_0_), channel_id=1, source_target_pairs={{0,2},{1,3},{2,0},{3,1},{4,6},{5,7},{6,4},{7,5},{8,10},{9,11},{10,... | collective-permute-start | bytes 24584 | tf_op jit(solution)/shard_map/ppermute | solution.py:320
  7.0 13.6 %collective-permute-start = (f32[16,128]{1,0:T(8,128)S(1)}, f32[16,128]{1,0:T(8,128)S(1)}, u32[]{:S(2)}, u32[]{:S(2)}) collective-permute-start(f32[16,128]{1,0:T(8,128)S(1)} %maximum_bitcast_fusion.refs_0_), channel_id=1, source_target_pairs={{0,1},{1,2},{2,3},{3,0},{4,5},{5,6},{6,7},{7,4},{8,9},{9,10},{10,1... | collective-permute-start | bytes 24584 | tf_op jit(solution)/shard_map/ppermute | solution.py:320
  8.3 12.2 %all-to-all-start = ((s32[8,1,128]{2,1,0:T(1,128)}), s32[8,1,128]{2,1,0:T(1,128)S(1)}, u32[]{:S(2)}, u32[]{:S(2)}) async-start(s32[8,1,128]{2,1,0:T(1,128)} %broadcast_select_fusion), calls=%async_computation | async-start | bytes 8192 | tf_op jit(solution)/shard_map/all_to_all | solution.py:308
  20.6 0.6 copy-start.3
  20.6 0.6 copy-start.4
  20.6 0.6 copy-start.5
  20.6 0.6 copy-start.6
  24.2 18.3 %all-to-all-start.1 = ((bf16[8,4,64,128]{3,2,1,0:T(8,128)(2,1)}), bf16[8,4,64,128]{3,2,1,0:T(8,128)(2,1)S(1)}, u32[]{:S(2)}, u32[]{:S(2)}) async-start(bf16[8,4,64,128]{3,2,1,0:T(8,128)(2,1)} %gather_far.1), calls=%async_computation.1 | async-start | bytes 1048576 | tf_op jit(solution)/shard_map/all_to_all | solution.py:338
  42.5 0.8 copy-start

commit v2 on v1

--- a/solution.py
+++ b/solution.py
@@ -81,128 +81,125 @@
     each(slots, normalize)
 
 
-def attend_kernel(full_width, head_step, parts, wanted, use_slot, *refs):
+def left_half():
+    return lax.broadcasted_iota(jnp.int32, (2 * TILE, HD), 1) < TILE
+
+
+def pick(x):
+    return jnp.where(left_half(), x[: 2 * TILE], x[2 * TILE :])
+
+
+def spread(x):
+    x = x.astype(jnp.float32)
+    zero = jnp.zeros_like(x)
+    left = left_half()
+    return jnp.concatenate(
+        (jnp.where(left, x, zero), jnp.where(left, zero, x)), axis=0
+    ).astype(jnp.bfloat16)
+
+
+def slots_of(use_slot, head, p):
+    return [use_slot[i, head * CAP + f] for i in (2 * p, 2 * p + 1) for f in range(CAP)]
+
+
+def far_tiles(far, slots, kind):
+    return jnp.concatenate([far[s // CAP, kind * CAP + s % CAP] for s in slots], axis=0)
+
+
+def near_kernel(full_width, parts, *refs):
     part_refs = refs[:parts]
-    (q_raw, k_raw, values, cot, q_gain, k_gain, mask, far,
-     attn, dq, dk, dv, far_grad, kept_k, kept_v,
-     kn, qn, s_scr, p_scr, ds_scr, fk_acc, fv_acc) = refs[parts:]
-    head = pl.program_id(0)
+    (q_raw, k_raw, values, cot, q_gain, k_gain, mask,
+     qn, kn_t, v_t, cot_t, exps, stat, kn) = refs[parts:]
     key_tokens = k_raw.shape[0]
     query_tokens = q_raw.shape[0]
-    key_tiles = key_tokens // TILE
-    pairs = query_tokens // HD
-    score_scale = 1.0 / math.sqrt(HD)
-    slots = far.shape[0] * CAP
+    exponent = LOG2E / math.sqrt(HD)
 
     inverse = inverse_rms(part_refs, full_width)
+    first = key_tokens // HD
+    for j in range(query_tokens // HD):
+        rows = slice(j * HD, (j + 1) * HD)
+        qn[rows, :] = (
+            q_raw[rows, :].astype(jnp.float32) * inverse[:, first + j : first + j + 1] * q_gain[0]
+        ).astype(jnp.bfloat16)
     for j in range(key_tokens // HD):
         rows = slice(j * HD, (j + 1) * HD)
         kn[rows, :] = (
             k_raw[rows, :].astype(jnp.float32) * inverse[:, j : j + 1] * k_gain[0]
         ).astype(jnp.bfloat16)
-    first = key_tokens // HD
-    for j in range(pairs):
-        rows = slice(j * HD, (j + 1) * HD)
-        qn[rows, :] = (
-            q_raw[rows, :].astype(jnp.float32) * inverse[:, first + j : first + j + 1] * q_gain[0]
-        ).astype(jnp.bfloat16)
+
+    step = 4 * TILE
+    top = None
+    for c in range(0, key_tokens, step):
+        block = dot(kn[c : c + step, :], qn[...], NT) * exponent
+        for t in range(step // TILE):
+            rows = slice(c + t * TILE, c + (t + 1) * TILE)
+            tile = block[t * TILE : (t + 1) * TILE] + mask[0, c // TILE + t, :][None]
+            exps[0, rows, :] = tile
+            tile = jnp.max(tile.reshape(TILE // 8, 8, query_tokens), axis=0)
+            top = tile if top is None else jnp.maximum(top, tile)
+    top = jnp.max(top, axis=0, keepdims=True)
+    total = jnp.zeros((8, query_tokens), jnp.float32)
+    for c in range(0, key_tokens, TILE):
+        e = jnp.exp2(exps[0, c : c + TILE, :] - top)
+        exps[0, c : c + TILE, :] = e
+        total = total + jnp.sum(e.reshape(TILE // 8, 8, query_tokens), axis=0)
+    stat[0, 0:1, :] = top
+    stat[0, 1:2, :] = jnp.sum(total, axis=0, keepdims=True)
+    kn_t[0] = kn[...].T
+    v_t[0] = values[...].T
+    cot_t[0] = cot[...].T
+
+
+def meet_kernel(use_slot, exps, stat, v_t, cot_t, cot, qn, far,
+                attn, probs, delta_out, far_ds_out, far_grad, fk_acc, fv_acc):
+    head = pl.program_id(0)
+    key_tokens, query_tokens = exps.shape[1:]
+    pairs = query_tokens // HD
+    score_scale = 1.0 / math.sqrt(HD)
+    slots = far.shape[0] * CAP
 
     @pl.when(head == 0)
     def _():
         fk_acc[...] = jnp.zeros_like(fk_acc)
         fv_acc[...] = jnp.zeros_like(fv_acc)
 
-    left = lax.broadcasted_iota(jnp.int32, (2 * TILE, HD), 1) < TILE
-    exponent = score_scale * LOG2E
-
-    def far_tiles(p, kind):
-        tiles = []
-        for i in (2 * p, 2 * p + 1):
-            for f in range(CAP):
-                s = use_slot[i, head * CAP + f]
-                tiles.append(far[s // CAP, kind * CAP + s % CAP])
-        return jnp.concatenate(tiles, axis=0)
-
-    def pick(x):
-        return jnp.where(left, x[: 2 * TILE], x[2 * TILE :])
-
-    def spread(x):
-        zero = jnp.zeros_like(x)
-        return jnp.concatenate((jnp.where(left, x, zero), jnp.where(left, zero, x)), axis=0)
-
-    top = None
-    for t in range(key_tiles):
-        rows = slice(t * TILE, (t + 1) * TILE)
-        block = dot(kn[rows, :], qn[...], NT) * exponent + mask[0, t : t + 1, :]
-        s_scr[rows, :] = block
-        block = jnp.max(block, axis=0, keepdims=True)
-        top = block if top is None else jnp.maximum(top, block)
-
+    far_v, far_e, used = [], [], []
+    scales = []
     for p in range(pairs):
         cols = slice(p * HD, (p + 1) * HD)
-        q_p = qn[cols, :]
+        used.append(slots_of(use_slot, head, p))
+        far_v.append(far_tiles(far, used[p], 1))
+        far_s = pick(dot(far_tiles(far, used[p], 0), qn[cols, :], NT)) * (score_scale * LOG2E)
+        near_top = stat[0, 0:1, cols]
+        top = jnp.maximum(near_top, jnp.max(far_s, axis=0, keepdims=True))
+        e = jnp.exp2(far_s - top)
+        shrink = jnp.exp2(near_top - top)
+        norm = 1.0 / (stat[0, 1:2, cols] * shrink + jnp.sum(e, axis=0, keepdims=True))
+        scales.append(shrink * norm)
+        far_e.append((e * norm).astype(jnp.bfloat16))
+    scale = jnp.concatenate(scales, axis=1)
+    for c in range(0, key_tokens, TILE):
+        probs[0, c : c + TILE, :] = (exps[0, c : c + TILE, :] * scale).astype(jnp.bfloat16)
+    out_t = dot(v_t[0], probs[0], NN)
+    for p in range(pairs):
+        cols = slice(p * HD, (p + 1) * HD)
         c_p = cot[cols, :]
-        far_k = far_tiles(p, 0)
-        far_v = far_tiles(p, 1)
-        far_s = pick(dot(far_k, q_p, NT)) * exponent
-        peak = jnp.maximum(top[:, cols], jnp.max(far_s, axis=0, keepdims=True))
-        far_e = jnp.exp2(far_s - peak)
-        total = jnp.sum(far_e, axis=0, keepdims=True)
-        for t in range(key_tiles):
-            rows = slice(t * TILE, (t + 1) * TILE)
-            e = jnp.exp2(s_scr[rows, cols] - peak)
-            s_scr[rows, cols] = e
-            total = total + jnp.sum(e, axis=0, keepdims=True)
-        norm = 1.0 / total
-        for t in range(key_tiles):
-            rows = slice(t * TILE, (t + 1) * TILE)
-            p_scr[rows, cols] = (s_scr[rows, cols] * norm).astype(jnp.bfloat16)
-        far_p = (far_e * norm).astype(jnp.bfloat16)
-        far_p4 = spread(far_p)
-        out_t = dot(values[...].T, p_scr[:, cols], NN) + dot(far_v.T, far_p4, NN)
-        out_b = out_t.astype(jnp.bfloat16)
+        far_p4 = spread(far_e[p])
+        out_b = (out_t[:, cols] + dot(far_v[p].T, far_p4, NN)).astype(jnp.bfloat16)
         attn[cols, :] = out_b.T
         delta = jnp.sum(
-            c_p.T.astype(jnp.float32) * out_b.astype(jnp.float32), axis=0, keepdims=True
+            cot_t[0, :, cols].astype(jnp.float32) * out_b.astype(jnp.float32),
+            axis=0, keepdims=True,
         )
-        far_dp = pick(dot(far_v, c_p, NT))
-        far_ds = (far_p.astype(jnp.float32) * (far_dp - delta) * score_scale).astype(jnp.bfloat16)
-        far_ds4 = spread(far_ds)
-        grad_k = dot(far_ds4, q_p, NN)
+        delta_out[0, 0:1, cols] = delta
+        far_dp = pick(dot(far_v[p], c_p, NT))
+        far_ds = (far_e[p].astype(jnp.float32) * (far_dp - delta) * score_scale).astype(jnp.bfloat16)
+        far_ds_out[0, :, cols] = far_ds
+        grad_k = dot(spread(far_ds), qn[cols, :], NN)
         grad_v = dot(far_p4, c_p, NN)
-        b = 0
-        for i in (2 * p, 2 * p + 1):
-            for f in range(CAP):
-                s = use_slot[i, head * CAP + f]
-                fk_acc[s] += grad_k[b * TILE : (b + 1) * TILE]
-                fv_acc[s] += grad_v[b * TILE : (b + 1) * TILE]
-                b += 1
-        for t in range(key_tiles):
-            rows = slice(t * TILE, (t + 1) * TILE)
-            dp = dot(values[rows, :], c_p, NT)
-            ds_scr[rows, cols] = (
-                p_scr[rows, cols].astype(jnp.float32) * (dp - delta) * score_scale
-            ).astype(jnp.bfloat16)
-        dq_t = dot(kn[...].T, ds_scr[:, cols], NN) + dot(far_k.T, far_ds4, NN)
-        dq[cols, :] = dq_t.astype(jnp.bfloat16).T
-
-    grad_k = dot(ds_scr[...], qn[...], NN)
-    grad_v = dot(p_scr[...], cot[...], NN)
-    dk[...] = grad_k.astype(jnp.bfloat16)
-    dv[...] = grad_v.astype(jnp.bfloat16)
-    s_scr[:, :HD] = grad_k
-    s_scr[:, HD : 2 * HD] = grad_v
-
-    def keep(s):
-        tile, owner = pair_of(wanted[s // CAP, s % CAP], head_step)
-
-        @pl.when(owner == head)
-        def _():
-            rows = pl.ds(pl.multiple_of(tile * TILE, TILE), TILE)
-            kept_k[s] = s_scr[rows, :HD]
-            kept_v[s] = s_scr[rows, HD : 2 * HD]
-
-    each(slots, keep)
+        for b, s in enumerate(used[p]):
+            fk_acc[s] += grad_k[b * TILE : (b + 1) * TILE]
+            fv_acc[s] += grad_v[b * TILE : (b + 1) * TILE]
 
     @pl.when(head == pl.num_programs(0) - 1)
     def _():
@@ -211,6 +208,44 @@
             far_grad[s // CAP, CAP + s % CAP] = fv_acc[s].astype(jnp.bfloat16)
 
         each(slots, send)
+
+
+def grad_kernel(head_step, wanted, use_slot, kn_t, qn, values, cot, probs, delta, far_ds, far,
+                dq, dk, dv, kept_k, kept_v, ds, acc_k, acc_v):
+    head = pl.program_id(0)
+    key_tokens, query_tokens = probs.shape[1:]
+    score_scale = 1.0 / math.sqrt(HD)
+    slots = far.shape[0] * CAP
+    step = 4 * TILE
+    for c in range(0, key_tokens, step):
+        rows = slice(c, c + step)
+        dp = dot(values[rows, :], cot[...], NT)
+        ds[rows, :] = (
+            probs[0, rows, :].astype(jnp.float32) * (dp - delta[0, 0:1, :]) * score_scale
+        ).astype(jnp.bfloat16)
+        grad_v = dot(probs[0, rows, :], cot[...], NN)
+        grad_k = dot(ds[rows, :], qn[...], NN)
+        acc_k[rows, :] = grad_k
+        acc_v[rows, :] = grad_v
+        dk[rows, :] = grad_k.astype(jnp.bfloat16)
+        dv[rows, :] = grad_v.astype(jnp.bfloat16)
+    dq_t = dot(kn_t[0], ds[...], NN)
+    for p in range(query_tokens // HD):
+        cols = slice(p * HD, (p + 1) * HD)
+        far_k = far_tiles(far, slots_of(use_slot, head, p), 0)
+        part = dq_t[:, cols] + dot(far_k.T, spread(far_ds[0, :, cols]), NN)
+        dq[cols, :] = part.astype(jnp.bfloat16).T
+
+    def keep(s):
+        tile, owner = pair_of(wanted[s // CAP, s % CAP], head_step)
+
+        @pl.when(owner == head)
+        def _():
+            rows = pl.ds(pl.multiple_of(tile * TILE, TILE), TILE)
+            kept_k[s] = acc_k[rows, :]
+            kept_v[s] = acc_v[rows, :]
+
+    each(slots, keep)
 
 
 def finish_kernel(head_step, wanted, back, kept_k, kept_v, dk_in, dv_in, dk, dv,
@@ -291,7 +326,7 @@
     full_width = local_width * group_count
     head_step = pl.next_power_of_2(head_count)
     slots = slab_count * CAP
-    vmem = pltpu.CompilerParams(vmem_limit_bytes=56 << 20)
+    vmem = pltpu.CompilerParams(vmem_limit_bytes=60 << 20)
 
     head_ids = jnp.arange(head_count, dtype=jnp.int32)[None, :, None]
     far_global = kept_tiles[:, :, NEAR:]
@@ -349,57 +384,125 @@
     def whole(*shape):
         return pl.BlockSpec(shape, lambda h, *_: (0,) * len(shape))
 
-    gain_spec = pl.BlockSpec((1, 1, HD), lambda h, *_: (h, 0, 0))
-    attn_out, dq_normed, dk, dv, far_grad, kept_k, kept_v = pl.pallas_call(
-        functools.partial(attend_kernel, full_width, head_step, group_count),
+    def each_head(*shape):
+        return pl.BlockSpec((1, *shape), lambda h, *_: (h,) + (0,) * len(shape))
+
+    def per_head(shape, dtype):
+        return jax.ShapeDtypeStruct((head_count, *shape), dtype)
+
+    def tokens_of(count):
+        return jax.ShapeDtypeStruct((count, local_width), jnp.bfloat16)
+
+    far_shape = (slab_count, 2 * CAP, TILE, HD)
+    qn, kn_t, v_t, cot_t, exps, stat = pl.pallas_call(
+        functools.partial(near_kernel, full_width, group_count),
+        grid=(head_count,),
+        in_specs=[whole(stat_rows, HD)] * group_count
+        + [
+            column(query_tokens),
+            column(key_tokens),
+            column(key_tokens),
+            column(query_tokens),
+            each_head(1, HD),
+            each_head(1, HD),
+            each_head(key_tiles, query_tokens),
+        ],
+        out_specs=[
+            column(query_tokens),
+            each_head(HD, key_tokens),
+            each_head(HD, key_tokens),
+            each_head(HD, query_tokens),
+            each_head(key_tokens, query_tokens),
+            each_head(8, query_tokens),
+        ],
+        out_shape=[
+            tokens_of(query_tokens),
+            per_head((HD, key_tokens), jnp.bfloat16),
+            per_head((HD, key_tokens), jnp.bfloat16),
+            per_head((HD, query_tokens), jnp.bfloat16),
+            per_head((key_tokens, query_tokens), jnp.float32),
+            per_head((8, query_tokens), jnp.float32),
+        ],
+        scratch_shapes=[pltpu.VMEM((key_tokens, HD), jnp.bfloat16)],
+        compiler_params=vmem,
+        name="near",
+    )(
+        *parts, q_raw, k_raw, values, cotangent,
+        q_gain.reshape(head_count, 1, HD), k_gain.reshape(head_count, 1, HD), mask,
+    )
+
+    attn_out, probs, delta, far_ds, far_grad = pl.pallas_call(
+        meet_kernel,
+        grid_spec=pltpu.PrefetchScalarGridSpec(
+            num_scalar_prefetch=1,
+            grid=(head_count,),
+            in_specs=[
+                each_head(key_tokens, query_tokens),
+                each_head(8, query_tokens),
+                each_head(HD, key_tokens),
+                each_head(HD, query_tokens),
+                column(query_tokens),
+                column(query_tokens),
+                whole(*far_shape),
+            ],
+            out_specs=[
+                column(query_tokens),
+                each_head(key_tokens, query_tokens),
+                each_head(8, query_tokens),
+                each_head(2 * TILE, query_tokens),
+                whole(*far_shape),
+            ],
+            scratch_shapes=[pltpu.VMEM((slots, TILE, HD), jnp.float32)] * 2,
+        ),
+        out_shape=[
+            tokens_of(query_tokens),
+            per_head((key_tokens, query_tokens), jnp.bfloat16),
+            per_head((8, query_tokens), jnp.float32),
+            per_head((2 * TILE, query_tokens), jnp.bfloat16),
+            jax.ShapeDtypeStruct(far_shape, jnp.bfloat16),
+        ],
+        compiler_params=vmem,
+        name="meet",
+    )(use_slot, exps, stat, v_t, cot_t, cotangent, qn, far)
+
+    dq_normed, dk, dv, kept_k, kept_v = pl.pallas_call(
+        functools.partial(grad_kernel, head_step),
         grid_spec=pltpu.PrefetchScalarGridSpec(
             num_scalar_prefetch=2,
             grid=(head_count,),
-            in_specs=[whole(stat_rows, HD)] * group_count
-            + [
+            in_specs=[
+                each_head(HD, key_tokens),
+                column(query_tokens),
+                column(key_tokens),
+                column(query_tokens),
+                each_head(key_tokens, query_tokens),
+                each_head(8, query_tokens),
+                each_head(2 * TILE, query_tokens),
+                whole(*far_shape),
+            ],
+            out_specs=[
                 column(query_tokens),
                 column(key_tokens),
                 column(key_tokens),
-                column(query_tokens),
-                gain_spec,
-                gain_spec,
-                pl.BlockSpec((1, key_tiles, query_tokens), lambda h, *_: (h, 0, 0)),
-                whole(slab_count, 2 * CAP, TILE, HD),
-            ],
-            out_specs=[
-                column(query_tokens),
-                column(query_tokens),
-                column(key_tokens),
-                column(key_tokens),
-                whole(slab_count, 2 * CAP, TILE, HD),
                 whole(slots, TILE, HD),
                 whole(slots, TILE, HD),
             ],
             scratch_shapes=[
-                pltpu.VMEM((key_tokens, HD), jnp.bfloat16),
-                pltpu.VMEM((query_tokens, HD), jnp.bfloat16),
-                pltpu.VMEM((key_tokens, query_tokens), jnp.float32),
                 pltpu.VMEM((key_tokens, query_tokens), jnp.bfloat16),
-                pltpu.VMEM((key_tokens, query_tokens), jnp.bfloat16),
-                pltpu.VMEM((slots, TILE, HD), jnp.float32),
-                pltpu.VMEM((slots, TILE, HD), jnp.float32),
+                pltpu.VMEM((key_tokens, HD), jnp.float32),
+                pltpu.VMEM((key_tokens, HD), jnp.float32),
             ],
         ),
         out_shape=[
-            jax.ShapeDtypeStruct((query_tokens, local_width), jnp.bfloat16),
-            jax.ShapeDtypeStruct((query_tokens, local_width), jnp.bfloat16),
-            jax.ShapeDtypeStruct((key_tokens, local_width), jnp.bfloat16),
-            jax.ShapeDtypeStruct((key_tokens, local_width), jnp.bfloat16),
-            jax.ShapeDtypeStruct((slab_count, 2 * CAP, TILE, HD), jnp.bfloat16),
+            tokens_of(query_tokens),
+            tokens_of(key_tokens),
+            tokens_of(key_tokens),
             jax.ShapeDtypeStruct((slots, TILE, HD), jnp.float32),
             jax.ShapeDtypeStruct((slots, TILE, HD), jnp.float32),
         ],
         compiler_params=vmem,
-        name="attend",
-    )(
-        wanted, use_slot, *parts, q_raw, k_raw, values, cotangent,
-        q_gain.reshape(head_count, 1, HD), k_gain.reshape(head_count, 1, HD), mask, far,
-    )
+        name="grad",
+    )(wanted, use_slot, kn_t, qn, values, cotangent, probs, delta, far_ds, far)
 
     back = lax.all_to_all(far_grad, "slab", split_axis=0, concat_axis=0, tiled=True)
     dk, dv = pl.pallas_call(

time: 101 us -> 80.2 us (0.79)
  blocking collectives: 18.4 us -> 0 us
  waiting for transfers between devices: 16.8 us -> 6.69 us
  starting transfers between devices: 12.6 us -> 17.4 us
  Pallas kernels: 41.3 us -> 43.4 us
    all_to_all x1 -> x0, blocking collectives: 18.4 us -> none  [local(): lax.all_to_all(far_grad, 'slab', split_axis=0, concat_axis=0, tiled=True)]
    all_to_all x1, waiting for transfers between devices: 11.7 us -> 1.09 us  [local(): lax.all_to_all(outgoing, 'slab', split_axis=0, concat_axis=0, tiled=True)]
    all_to_all x0 -> x1, starting transfers between devices: none -> 4.86 us  [local(): lax.all_to_all(far_grad, 'slab', split_axis=0, concat_axis=0, tiled=True)]
    pallas_call x1 -> x3, Pallas kernels: 35.5 us -> 37.5 us  [the longest x1 13.8 us: local(): pl.pallas_call(functools.partial(grad_kernel, head_step), grid_spec=pltpu...]
    unnamed x18 -> x20, local copies, waits for them, and re-layouts: 1.38 us -> 2.23 us
  transfers between devices with their start and end apart: 5 -> 6, of which waited for: 2 -> 3; matrix products, arithmetic and copies ran while one was open for 5% -> 7% of each run, Pallas kernels for 0% -> 31%
where the time goes in v2:
time: 80.2 us; the launch traced here: 79.2 us
  Pallas kernels  43.4 us (54%)
  starting transfers between devices  17.4 us (22%)
  waiting for transfers between devices  6.69 us (8%)
  local copies, waits for them, and re-layouts  6.57 us (8%)
  other arithmetic  4.28 us (5%)
  between operations  0.83 us (1%)
    pallas_call x1, Pallas kernels, local(): pl.pallas_call(functools.partial(grad_kernel, head_step), grid_spec=pltpu...  13.8 us
    pallas_call x1, Pallas kernels, local(): pl.pallas_call(meet_kernel, grid_spec=pltpu.PrefetchScalarGridSpec(num_sc...  13.3 us
    pallas_call x1, Pallas kernels, local(): pl.pallas_call(functools.partial(near_kernel, full_width, group_count), g...  10.5 us
    all_to_all x1, starting transfers between devices, local(): lax.all_to_all(request, 'slab', split_axis=0, concat_axis=0, tiled=True)  5.84 us
    all_to_all x1, waiting for transfers between devices, local(): lax.all_to_all(request, 'slab', split_axis=0, concat_axis=0, tiled=True)  5.19 us
    all_to_all x1, starting transfers between devices, local(): lax.all_to_all(far_grad, 'slab', split_axis=0, concat_axis=0, tiled=True)  4.86 us
    all_to_all x1, starting transfers between devices, local(): lax.all_to_all(outgoing, 'slab', split_axis=0, concat_axis=0, tiled=True)  3.51 us
    ppermute x3, starting transfers between devices, local(): lax.ppermute(stats, 'head', [(i, (i + step) % group_count) for i in range...  3.23 us
  transfers between devices with their start and end apart: 6, of which 3 were waited for; matrix products, arithmetic and copies ran while one was open for 7% of the time, Pallas kernels for 31%

profile of v2, /device:TPU:0, one launch (start us, length us, event | category | flops | bytes accessed | tf_op | source)
XLA Modules:
  0.0 79.2 jit_solution(12193433234028005880)
XLA Ops:
  0.7 1.2 %multiply_reduce_fusion.1 = f32[384]{0:T(512)S(1)} fusion(bf16[384,640]{1,0:T(8,128)(2,1)} %refs_4_.1), kind=kLoop, calls=%fused_computation.2 | loop fusion | flops 736896 | bytes 493056 | tf_op jit(solution)/shard_map/reduce_sum | solution.py:348
  1.9 2.0 %multiply_reduce_fusion = f32[1536]{0:T(1024)S(1)} fusion(bf16[1536,640]{1,0:T(8,128)(2,1)} %refs_5_.3), kind=kLoop, calls=%fused_computation.1 | loop fusion | flops 2947584 | bytes 1972224 | tf_op jit(solution)/shard_map/reduce_sum | solution.py:347
  3.9 2.4 %collective-permute-start.2 = (f32[16,128]{1,0:T(8,128)S(1)}, f32[16,128]{1,0:T(8,128)S(1)}, u32[]{:S(2)}, u32[]{:S(2)}) collective-permute-start(f32[16,128]{1,0:T(8,128)S(1)} %maximum_bitcast_fusion.refs_0_), channel_id=1, source_target_pairs={{0,3},{1,0},{2,1},{3,2},{4,7},{5,4},{6,5},{7,6},{8,11},{9,8},{10,9... | collective-permute-start | bytes 24584 | tf_op jit(solution)/shard_map/ppermute | solution.py:355
  6.3 0.6 collective-permute-start.1
  7.0 0.2 collective-permute-start
  7.3 0.1 broadcast_in_dim.72
  7.4 0.1 eq.48
  7.5 0.2 select_reduce_fusion
  7.7 0.7 broadcast_select_fusion
  8.3 5.8 %all-to-all-start = ((s32[8,1,128]{2,1,0:T(1,128)}), s32[8,1,128]{2,1,0:T(1,128)S(1)}, u32[]{:S(2)}, u32[]{:S(2)}) async-start(s32[8,1,128]{2,1,0:T(1,128)} %broadcast_select_fusion), calls=%async_computation | async-start | bytes 8192 | tf_op jit(solution)/shard_map/all_to_all | solution.py:343
  14.2 0.6 reshape.101.refs_8_
  14.8 0.6 reshape.102.refs_9_
  15.4 5.2 %all-to-all-done = s32[8,1,128]{2,1,0:T(1,128)S(1)} async-done(((s32[8,1,128]{2,1,0:T(1,128)}), s32[8,1,128]{2,1,0:T(1,128)S(1)}, u32[]{:S(2)}, u32[]{:S(2)}) %all-to-all-start) | async-done | bytes 4128 | tf_op jit(solution)/shard_map/all_to_all | solution.py:343
  20.6 0.5 copy-done.4
  21.2 3.1 %gather_far.1 = bf16[8,4,64,128]{3,2,1,0:T(8,128)(2,1)} custom-call(s32[8,128]{1,0:T(8,128)} %bitcast.6, f32[16,128]{1,0:T(8,128)} %copy-done.3, f32[16,128]{1,0:T(8,128)} %copy-done.7, f32[16,128]{1,0:T(8,128)} %copy-done.6, f32[16,128]{1,0:T(8,128)} %copy-done.5, f32[5,128]{1,0:T(8,128)} %bitcast.9, bf16[1536,640]{1,0:T(8,128)(2,1)} %refs_5_.3, ...), custom_call_target="tpu_custom_call" | custom-call | tf_op jit(solution)/shard_map/gather_far/pallas_call | solution.py:360
  24.3 3.5 %all-to-all-start.1 = ((bf16[8,4,64,128]{3,2,1,0:T(8,128)(2,1)}), bf16[8,4,64,128]{3,2,1,0:T(8,128)(2,1)S(1)}, u32[]{:S(2)}, u32[]{:S(2)}) async-start(bf16[8,4,64,128]{3,2,1,0:T(8,128)(2,1)} %gather_far.1), calls=%async_computation.1 | async-start | bytes 1048576 | tf_op jit(solution)/shard_map/all_to_all | solution.py:373
  27.9 0.1 copy.30
  28.0 0.1 fusion
  28.1 0.1 copy.31
  28.4 0.8 gather_fusion
  29.3 0.7 reshape.115.use_slot
  29.9 0.2 broadcast_in_dim.80
  30.1 0.8 %reshape.103.refs_10_ = f32[5,24,384]{2,1,0:T(8,128)} reshape(f32[5,24,6,64]{3,2,1,0:T(8,128)S(1)} %broadcast_in_dim.80) | data formatting | bytes 368640 | tf_op jit(solution)/shard_map/reshape | solution.py:379
  31.0 10.5 %near.1 = (bf16[384,640]{1,0:T(8,128)(2,1)}, bf16[5,128,1536]{2,1,0:T(8,128)(2,1)}, bf16[5,128,1536]{2,1,0:T(8,128)(2,1)}, bf16[5,128,384]{2,1,0:T(8,128)(2,1)},...) custom-call(f32[16,128]{1,0:T(8,128)} %copy-done.3, f32[16,128]{1,0:T(8,128)} %copy-done.7, f32[16,128]{1,0:T(8,128)} %copy-done.6, ...), custom_call_target="tpu_custom_call" | custom-call | tf_op jit(solution)/shard_map/near/pallas_call | solution.py:397
  41.4 1.1 %all-to-all-done.1.far = bf16[8,4,64,128]{3,2,1,0:T(8,128)(2,1)S(1)} async-done(((bf16[8,4,64,128]{3,2,1,0:T(8,128)(2,1)}), bf16[8,4,64,128]{3,2,1,0:T(8,128)(2,1)S(1)}, u32[]{:S(2)}, u32[]{:S(2)}) %all-to-all-start.1) | async-done | bytes 524320 | tf_op jit(solution)/shard_map/all_to_all | solution.py:373
  42.5 0.8 %copy-done = bf16[8,4,64,128]{3,2,1,0:T(8,128)(2,1)} copy-done((bf16[8,4,64,128]{3,2,1,0:T(8,128)(2,1)}, bf16[8,4,64,128]{3,2,1,0:T(8,128)(2,1)S(1)}, u32[]{:S(2)}) %copy-start) | copy-done | bytes 524312
  43.3 13.3 %meet.1 = (bf16[384,640]{1,0:T(8,128)(2,1)}, bf16[5,1536,384]{2,1,0:T(8,128)(2,1)}, f32[5,8,384]{2,1,0:T(8,128)}, bf16[5,128,384]{2,1,0:T(8,128)(2,1)}, bf16[8,4,64,128]{3,2,1,0:T(8,128)(2,1)}) custom-call(s32[6,10]{1,0:T(8,128)} %reshape.115.use_slot, f32[5,1536,384]{2,1,0:T(8,128)} %get-tuple-element.22.exps, f32[5,8,384]{2,1,0:T(8,128)} %get-tuple-element.23.stat, ...), custom_call_target="tpu_custom_call" | custom-call | tf_op jit(solution)/shard_map/meet/pallas_call | solution.py:434
  56.6 4.9 %all-to-all-start.2 = ((bf16[8,4,64,128]{3,2,1,0:T(8,128)(2,1)}), bf16[8,4,64,128]{3,2,1,0:T(8,128)(2,1)S(1)}, u32[]{:S(2)}, u32[]{:S(2)}) async-start(bf16[8,4,64,128]{3,2,1,0:T(8,128)(2,1)} %get-tuple-element.33), calls=%async_computation.2 | async-start | bytes 1048576 | tf_op jit(solution)/shard_map/all_to_all | solution.py:507
  61.5 13.8 %grad.1 = (bf16[384,640]{1,0:T(8,128)(2,1)}, bf16[1536,640]{1,0:T(8,128)(2,1)}, bf16[1536,640]{1,0:T(8,128)(2,1)}, f32[16,64,128]{2,1,0:T(8,128)}, f32[16,64,128]{2,1,0:T(8,128)}) custom-call(s32[8,128]{1,0:T(8,128)} %bitcast.7, s32[6,10]{1,0:T(8,128)} %reshape.115.use_slot, bf16[5,128,1536]{2,1,0:T(8,128)(2,1)} %get-tuple-element.28.kn_t, ...), custom_call_target="tpu_custom_call" | custom-call | tf_op jit(solution)/shard_map/grad/pallas_call | solution.py:468
  75.3 0.4 all-to-all-done.2.back
  75.7 0.8 %copy-done.1 = bf16[8,4,64,128]{3,2,1,0:T(8,128)(2,1)} copy-done((bf16[8,4,64,128]{3,2,1,0:T(8,128)(2,1)}, bf16[8,4,64,128]{3,2,1,0:T(8,128)(2,1)S(1)}, u32[]{:S(2)}) %copy-start.1) | copy-done | bytes 524312
  76.5 2.7 %finish.1 = (bf16[1536,640]{1,0:T(8,128)(2,1)}, bf16[1536,640]{1,0:T(8,128)(2,1)}) custom-call(s32[8,128]{1,0:T(8,128)} %bitcast.8, bf16[8,4,64,128]{3,2,1,0:T(8,128)(2,1)} %copy-done.1, f32[16,64,128]{2,1,0:T(8,128)} %get-tuple-element.34.kept_k, f32[16,64,128]{2,1,0:T(8,128)} %get-tuple-element.35.kept_v, ...), custom_call_target="tpu_custom_call", output_to_operand_aliasing={{0}: (4, {}), {1}: (5, {})} | custom-call | tf_op jit(solution)/shard_map/finish/pallas_call | solution.py:508
  (32 shorter events, 0.4 us)
Async XLA Ops:
  0.6 6.5 %copy-start.2 = (s32[6,5,12]{2,0,1:T(8,128)S(1)}, s32[6,5,12]{2,0,1:T(8,128)}, u32[]{:S(2)}) copy-start(s32[6,5,12]{2,0,1:T(8,128)} %param.13) | copy-start | bytes 4324
  0.6 13.5 %copy-start.9 = (f32[640]{0:T(1024)S(1)}, f32[640]{0:T(1024)}, u32[]{:S(2)}) copy-start(f32[640]{0:T(1024)} %param.10) | copy-start | bytes 7684
  0.7 14.1 %copy-start.8 = (f32[640]{0:T(1024)S(1)}, f32[640]{0:T(1024)}, u32[]{:S(2)}) copy-start(f32[640]{0:T(1024)} %param.11) | copy-start | bytes 7684
  3.9 16.7 %copy-start.3 = (f32[16,128]{1,0:T(8,128)}, f32[16,128]{1,0:T(8,128)S(1)}, u32[]{:S(2)}) copy-start(f32[16,128]{1,0:T(8,128)S(1)} %maximum_bitcast_fusion.refs_0_) | copy-start | bytes 24580
  3.9 16.6 %collective-permute-start.2 = (f32[16,128]{1,0:T(8,128)S(1)}, f32[16,128]{1,0:T(8,128)S(1)}, u32[]{:S(2)}, u32[]{:S(2)}) collective-permute-start(f32[16,128]{1,0:T(8,128)S(1)} %maximum_bitcast_fusion.refs_0_), channel_id=1, source_target_pairs={{0,3},{1,0},{2,1},{3,2},{4,7},{5,4},{6,5},{7,6},{8,11},{9,8},{10,9... | collective-permute-start | bytes 24584 | tf_op jit(solution)/shard_map/ppermute | solution.py:355
  6.3 14.2 %collective-permute-start.1 = (f32[16,128]{1,0:T(8,128)S(1)}, f32[16,128]{1,0:T(8,128)S(1)}, u32[]{:S(2)}, u32[]{:S(2)}) collective-permute-start(f32[16,128]{1,0:T(8,128)S(1)} %maximum_bitcast_fusion.refs_0_), channel_id=1, source_target_pairs={{0,2},{1,3},{2,0},{3,1},{4,6},{5,7},{6,4},{7,5},{8,10},{9,11},{10,... | collective-permute-start | bytes 24584 | tf_op jit(solution)/shard_map/ppermute | solution.py:355
  7.0 13.6 %collective-permute-start = (f32[16,128]{1,0:T(8,128)S(1)}, f32[16,128]{1,0:T(8,128)S(1)}, u32[]{:S(2)}, u32[]{:S(2)}) collective-permute-start(f32[16,128]{1,0:T(8,128)S(1)} %maximum_bitcast_fusion.refs_0_), channel_id=1, source_target_pairs={{0,1},{1,2},{2,3},{3,0},{4,5},{5,6},{6,7},{7,4},{8,9},{9,10},{10,1... | collective-permute-start | bytes 24584 | tf_op jit(solution)/shard_map/ppermute | solution.py:355
  8.3 12.2 %all-to-all-start = ((s32[8,1,128]{2,1,0:T(1,128)}), s32[8,1,128]{2,1,0:T(1,128)S(1)}, u32[]{:S(2)}, u32[]{:S(2)}) async-start(s32[8,1,128]{2,1,0:T(1,128)} %broadcast_select_fusion), calls=%async_computation | async-start | bytes 8192 | tf_op jit(solution)/shard_map/all_to_all | solution.py:343
  20.6 0.6 copy-start.4
  20.6 0.6 copy-start.5
  20.6 0.6 copy-start.6
  20.6 0.6 copy-start.7
  24.3 18.2 %all-to-all-start.1 = ((bf16[8,4,64,128]{3,2,1,0:T(8,128)(2,1)}), bf16[8,4,64,128]{3,2,1,0:T(8,128)(2,1)S(1)}, u32[]{:S(2)}, u32[]{:S(2)}) async-start(bf16[8,4,64,128]{3,2,1,0:T(8,128)(2,1)} %gather_far.1), calls=%async_computation.1 | async-start | bytes 1048576 | tf_op jit(solution)/shard_map/all_to_all | solution.py:373
  42.5 0.8 %copy-start = (bf16[8,4,64,128]{3,2,1,0:T(8,128)(2,1)}, bf16[8,4,64,128]{3,2,1,0:T(8,128)(2,1)S(1)}, u32[]{:S(2)}) copy-start(bf16[8,4,64,128]{3,2,1,0:T(8,128)(2,1)S(1)} %all-to-all-done.1.far) | copy-start | bytes 1572868
  56.6 19.0 %all-to-all-start.2 = ((bf16[8,4,64,128]{3,2,1,0:T(8,128)(2,1)}), bf16[8,4,64,128]{3,2,1,0:T(8,128)(2,1)S(1)}, u32[]{:S(2)}, u32[]{:S(2)}) async-start(bf16[8,4,64,128]{3,2,1,0:T(8,128)(2,1)} %get-tuple-element.33), calls=%async_computation.2 | async-start | bytes 1048576 | tf_op jit(solution)/shard_map/all_to_all | solution.py:507
  75.7 0.8 %copy-start.1 = (bf16[8,4,64,128]{3,2,1,0:T(8,128)(2,1)}, bf16[8,4,64,128]{3,2,1,0:T(8,128)(2,1)S(1)}, u32[]{:S(2)}) copy-start(bf16[8,4,64,128]{3,2,1,0:T(8,128)(2,1)S(1)} %all-to-all-done.2.back) | copy-start | bytes 1572868

commit v3 on v2

v3 whole, which is shorter than its diff:
```python
import functools
import math

import jax
import jax.numpy as jnp
from jax import lax
from jax.experimental import pallas as pl
from jax.experimental.pallas import tpu as pltpu
from jax.sharding import PartitionSpec as P

TILE = 64
NEAR = 10
CAP = 2
HD = 128

NORM_EPSILON = 1e-06
MASKED = -1e30

VMEM = pl.BlockSpec(memory_space=pltpu.VMEM)
SMEM = pl.BlockSpec(memory_space=pltpu.SMEM)
HBM = pl.BlockSpec(memory_space=pltpu.HBM)
ANYWHERE = pl.BlockSpec(memory_space=pl.ANY)
LIMIT = 1 << 20
NT = (((1,), (1,)), ((), ()))
NN = (((1,), (0,)), ((), ()))
LOG2E = math.log2(math.e)


def dot(a, b, dims):
    return lax.dot_general(a, b, dims, preferred_element_type=jnp.float32)


def each(count, body):
    if count <= 16:
        for i in range(count):
            body(i)
    else:
        lax.fori_loop(0, count, lambda i, c: (body(i), c)[1], 0)


def inverse_rms(part_refs, full_width):
    total = part_refs[0][...]
    for ref in part_refs[1:]:
        total = total + ref[...]
    return lax.rsqrt(total / full_width + NORM_EPSILON).T


def pair_of(wanted, s, head_step):
    code = wanted[s // CAP, s % CAP]
    return lax.shift_right_logical(code, head_step.bit_length() - 1), code & (head_step - 1)


def gather_kernel(full_width, head_step, parts, wanted, *refs):
    part_refs, (gain, k_raw, values, out, k_buf, v_buf, k_out, scale, sems) = (
        refs[:parts],
        refs[parts:],
    )
    slots = out.shape[0] * CAP

    def source(s):
        tile, head = pair_of(wanted, s, head_step)
        return (
            pl.ds(pl.multiple_of(tile * TILE, TILE), TILE),
            pl.ds(pl.multiple_of(head * HD, HD), HD),
        )

    def k_in(s):
        return pltpu.make_async_copy(k_raw.at[source(s)], k_buf.at[s], sems.at[0, s])

    def v_in(s):
        return pltpu.make_async_copy(values.at[source(s)], v_buf.at[s], sems.at[1, s])

    def k_copy(s):
        return pltpu.make_async_copy(k_out.at[s], out.at[s // CAP, s % CAP], sems.at[2, s])

    def v_copy(s):
        return pltpu.make_async_copy(v_buf.at[s], out.at[s // CAP, CAP + s % CAP], sems.at[3, s])

    each(slots, lambda s: v_in(s).start())
    each(slots, lambda s: k_in(s).start())
    inverse = inverse_rms(part_refs, full_width)
    for j in range(scale.shape[0] // HD):
        scale[j * HD : (j + 1) * HD, :] = jnp.broadcast_to(inverse[:, j : j + 1], (HD, HD))

    def normalize(s):
        rows, cols = source(s)
        k_in(s).wait()
        k_out[s] = (k_buf[s].astype(jnp.float32) * scale[rows, :] * gain[cols][None]).astype(
            jnp.bfloat16
        )
        k_copy(s).start()

    def forward(s):
        v_in(s).wait()
        v_copy(s).start()

    each(slots, forward)
    each(slots, normalize)
    each(slots, lambda s: v_copy(s).wait())
    each(slots, lambda s: k_copy(s).wait())


def left_half():
    return lax.broadcasted_iota(jnp.int32, (2 * TILE, HD), 1) < TILE


def pick(x):
    return jnp.where(left_half(), x[: 2 * TILE], x[2 * TILE :])


def slots_of(kept, request, key_tiles, head_step, head, p):
    slots = []
    for i in (2 * p, 2 * p + 1):
        for f in range(CAP):
            tile = kept[i, head * (NEAR + CAP) + NEAR + f]
            owner = lax.div(tile, key_tiles)
            code = (tile - owner * key_tiles) * head_step + head
            slots.append(owner * CAP + jnp.where(request[owner, 0] == LIMIT - code, 0, 1))
    return slots


def far_tiles(far, slots, first=0):
    return jnp.concatenate([far[s // CAP, first + s % CAP] for s in slots], axis=0)


def halves_t(tiles):
    return jnp.concatenate((tiles[: 2 * TILE].T, tiles[2 * TILE :].T), axis=0)


def split_rows(x):
    zero = jnp.zeros((TILE, x.shape[1]), x.dtype)
    return jnp.concatenate(
        (
            jnp.concatenate((x[:TILE], zero), axis=0),
            jnp.concatenate((zero, x[TILE:]), axis=0),
        ),
        axis=1,
    )


def near_kernel(full_width, parts, *refs):
    part_refs = refs[:parts]
    (q_raw, k_raw, values, cot, q_gain, k_gain, mask,
     kn, qn, kn_t, v_t, cot_t, stat, scores) = refs[parts:]
    key_tokens = k_raw.shape[0]
    query_tokens = q_raw.shape[0]
    exponent = LOG2E / math.sqrt(HD)

    inverse = inverse_rms(part_refs, full_width)
    first = key_tokens // HD
    for j in range(query_tokens // HD):
        rows = slice(j * HD, (j + 1) * HD)
        qn[rows, :] = (
            q_raw[rows, :].astype(jnp.float32) * inverse[:, first + j : first + j + 1] * q_gain[...]
        ).astype(jnp.bfloat16)
    for j in range(key_tokens // HD):
        rows = slice(j * HD, (j + 1) * HD)
        kn[rows, :] = (
            k_raw[rows, :].astype(jnp.float32) * inverse[:, j : j + 1] * k_gain[...]
        ).astype(jnp.bfloat16)

    step = 4 * TILE
    top = None
    for c in range(0, key_tokens, step):
        block = dot(kn[c : c + step, :], qn[...], NT) * exponent
        for t in range(step // TILE):
            rows = slice(c + t * TILE, c + (t + 1) * TILE)
            tile = block[t * TILE : (t + 1) * TILE] + mask[0, c // TILE + t, :][None]
            scores[rows, :] = tile
            tile = jnp.max(tile.reshape(TILE // 8, 8, query_tokens), axis=0)
            top = tile if top is None else jnp.maximum(top, tile)
    top = jnp.max(top, axis=0, keepdims=True)
    total = jnp.zeros((8, query_tokens), jnp.float32)
    for c in range(0, key_tokens, TILE):
        e = jnp.exp2(scores[c : c + TILE, :] - top)
        total = total + jnp.sum(e.reshape(TILE // 8, 8, query_tokens), axis=0)
    stat[0, 0:1, :] = top
    stat[0, 1:2, :] = jnp.sum(total, axis=0, keepdims=True)
    kn_t[0] = kn[...].T
    v_t[0] = values[...].T
    cot_t[0] = cot[...].T


def meet_kernel(head_step, kept, request, kn_in, qn_in, stat_in, mask_in, v_t_in, cot_t_in, cot_in,
                far_in, attn_out, probs_out, delta_out, far_ds_out, far_k_out, far_grad_out,
                far, kn, qn, stat, mask, v_t, cot_t, cot, attn, probs, delta, far_ds, far_p, outs,
                logs, k_acc, v_acc, far_grad, in_sems, out_sems):
    heads, key_tiles, query_tokens = mask.shape
    pairs = query_tokens // HD
    score_scale = 1.0 / math.sqrt(HD)
    exponent = score_scale * LOG2E
    slots = far.shape[0] * CAP

    def lanes(h):
        return slice(h * HD, (h + 1) * HD)

    fetches = [
        [
            pltpu.make_async_copy(src, dst, in_sems.at[h, n])
            for n, (src, dst) in enumerate(
                (
                    (qn_in.at[:, lanes(h)], qn.at[:, lanes(h)]),
                    (stat_in.at[h], stat.at[h]),
                    (mask_in.at[h], mask.at[h]),
                    (kn_in.at[:, lanes(h)], kn.at[:, lanes(h)]),
                    (v_t_in.at[h], v_t.at[h]),
                    (cot_t_in.at[h], cot_t.at[h]),
                    (cot_in.at[:, lanes(h)], cot.at[:, lanes(h)]),
                )
            )
        ]
        for h in range(heads)
    ]
    fetch_far = pltpu.make_async_copy(far_in, far, in_sems.at[heads, 0])
    fetch_far.start()
    for first, last in ((0, 2), (2, 5), (5, 7)):
        for h in range(heads):
            for copy in fetches[h][first:last]:
                copy.start()
    stores = []
    k_acc[...] = jnp.zeros_like(k_acc)
    v_acc[...] = jnp.zeros_like(v_acc)
    used = [
        [slots_of(kept, request, key_tiles, head_step, h, p) for p in range(pairs)]
        for h in range(heads)
    ]

    def far_scores(h):
        for copy in fetches[h][:2]:
            copy.wait()
        for p in range(pairs):
            cols = slice(p * HD, (p + 1) * HD)
            far_s = pick(dot(far_tiles(far, used[h][p]), qn[cols, lanes(h)], NT)) * exponent
            near_top = stat[h, 0:1, cols]
            top = jnp.maximum(near_top, jnp.max(far_s, axis=0, keepdims=True))
            total = stat[h, 1:2, cols] * jnp.exp2(near_top - top) + jnp.sum(
                jnp.exp2(far_s - top), axis=0, keepdims=True
            )
            log_total = top + jnp.log2(total)
            logs[h, 0:1, cols] = log_total
            far_p[h, :, cols] = jnp.exp2(far_s - log_total).astype(jnp.bfloat16)

    step = 4 * TILE

    def near_part(h):
        for copy in fetches[h][2:5]:
            copy.wait()
        for c in range(0, key_tiles * TILE, step):
            block = dot(kn[c : c + step, lanes(h)], qn[:, lanes(h)], NT) * exponent
            for t in range(step // TILE):
                row = mask[h, c // TILE + t, :][None] - logs[h, 0:1, :]
                probs[h, c + t * TILE : c + (t + 1) * TILE, :] = jnp.exp2(
                    block[t * TILE : (t + 1) * TILE] + row
                ).astype(jnp.bfloat16)
        outs[h] = dot(v_t[h], probs[h], NN)
        stores.append(pltpu.make_async_copy(probs.at[h], probs_out.at[h], out_sems.at[h]))
        stores[-1].start()

    def far_part(h):
        for copy in fetches[h][5:]:
            copy.wait()
        for p in range(pairs):
            cols = slice(p * HD, (p + 1) * HD)
            values = far_tiles(far, used[h][p], CAP)
            weights = far_p[h, :, cols]
            out_b = (outs[h, :, cols] + pick(dot(halves_t(values), weights, NN))).astype(
                jnp.bfloat16
            )
            attn[cols, lanes(h)] = out_b.T
            row_delta = jnp.sum(
                cot_t[h, :, cols].astype(jnp.float32) * out_b.astype(jnp.float32),
                axis=0, keepdims=True,
            )
            delta[h, 0:1, cols] = row_delta
            grad_p = pick(dot(values, cot[cols, lanes(h)], NT))
            ds = (weights.astype(jnp.float32) * (grad_p - row_delta) * score_scale).astype(
                jnp.bfloat16
            )
            far_ds[h, :, cols] = ds
            grad_k = dot(ds, split_rows(qn[cols, lanes(h)]), NN)
            grad_v = dot(weights, split_rows(cot[cols, lanes(h)]), NN)
            for n, s in enumerate(used[h][p]):
                rows = slice(n % CAP * TILE, (n % CAP + 1) * TILE)
                half = slice(n // CAP * HD, (n // CAP + 1) * HD)
                k_acc[s] += grad_k[rows, half]
                v_acc[s] += grad_v[rows, half]

    fetch_far.wait()
    stores.append(pltpu.make_async_copy(far.at[:, :CAP], far_k_out, out_sems.at[heads]))
    stores[-1].start()
    for h in range(heads):
        far_scores(h)
    near_part(0)
    for h in range(1, heads):
        near_part(h)
        far_part(h - 1)
    far_part(heads - 1)

    def send(s):
        far_grad[s // CAP, s % CAP] = k_acc[s].astype(jnp.bfloat16)
        far_grad[s // CAP, CAP + s % CAP] = v_acc[s].astype(jnp.bfloat16)

    each(slots, send)
    for n, (src, dst) in enumerate(
        ((far_grad, far_grad_out), (attn, attn_out), (delta, delta_out), (far_ds, far_ds_out))
    ):
        stores.append(pltpu.make_async_copy(src, dst, out_sems.at[heads + 1 + n]))
        stores[-1].start()
    for copy in stores:
        copy.wait()


def grad_kernel(head_step, kept, request, wanted, kn_t_in, qn_in, values_in, cot_in, probs_in,
                delta_in, far_ds_in, far_k_in, dq_out, dk_out, dv_out, tiles_out,
                kn_t, qn, values, cot, pair, delta, far_ds, far_k, weights, acc,
                dq, dk, dv, in_sems, out_sems, tile_sems):
    heads, key_tokens = pair.shape[:2]
    query_tokens = qn.shape[0]
    score_scale = 1.0 / math.sqrt(HD)
    slots = far_k.shape[0] * CAP
    step = 4 * TILE

    def lanes(h):
        return slice(h * HD, (h + 1) * HD)

    fetches = [
        [
            pltpu.make_async_copy(src, dst, in_sems.at[h, n])
            for n, (src, dst) in enumerate(
                (
                    (values_in.at[:, lanes(h)], values.at[:, lanes(h)]),
                    (cot_in.at[:, lanes(h)], cot.at[:, lanes(h)]),
                    (probs_in.at[h], pair.at[h, :, query_tokens:]),
                    (delta_in.at[h], delta.at[h]),
                    (qn_in.at[:, lanes(h)], qn.at[:, lanes(h)]),
                    (kn_t_in.at[h], kn_t.at[h]),
                    (far_ds_in.at[h], far_ds.at[h]),
                )
            )
        ]
        for h in range(heads)
    ]
    far_fetch = pltpu.make_async_copy(far_k_in, far_k, in_sems.at[heads, 0])
    for first, last in ((0, 5), (5, 7)):
        for h in range(heads):
            for copy in fetches[h][first:last]:
                copy.start()
    far_fetch.start()
    weights[...] = jnp.zeros_like(weights)
    stores = []
    for h in range(heads):
        for copy in fetches[h][:5]:
            copy.wait()
        weights[h % 2, :query_tokens, :HD] = qn[:, lanes(h)]
        weights[h % 2, query_tokens:, HD:] = cot[:, lanes(h)]
        for c in range(0, key_tokens, step):
            rows = slice(c, c + step)
            dp = dot(values[rows, lanes(h)], cot[:, lanes(h)], NT)
            pair[h, rows, :query_tokens] = (
                pair[h, rows, query_tokens:].astype(jnp.float32)
                * (dp - delta[h, 0:1, :])
                * score_scale
            ).astype(jnp.bfloat16)
        for c in range(0, key_tokens, step):
            rows = slice(c, c + step)
            both = dot(pair[h, rows, :], weights[h % 2], NN)
            acc[h, rows, :] = both
            dk[rows, lanes(h)] = both[:, :HD].astype(jnp.bfloat16)
            dv[rows, lanes(h)] = both[:, HD:].astype(jnp.bfloat16)
        for n, (src, dst) in enumerate(((dk, dk_out), (dv, dv_out))):
            stores.append(
                pltpu.make_async_copy(
                    src.at[:, lanes(h)], dst.at[:, lanes(h)], out_sems.at[h, n]
                )
            )
            stores[-1].start()

    def keep(s):
        tile, owner = pair_of(wanted, s, head_step)
        rows = pl.ds(pl.multiple_of(tile * TILE, TILE), TILE)
        return pltpu.make_async_copy(acc.at[owner, rows, :], tiles_out.at[s], tile_sems.at[s])

    each(slots, lambda s: keep(s).start())
    far_fetch.wait()
    for h in range(heads):
        for copy in fetches[h][5:]:
            copy.wait()
        dq_t = dot(kn_t[h], pair[h, :, :query_tokens], NN)
        for p in range(query_tokens // HD):
            cols = slice(p * HD, (p + 1) * HD)
            used = slots_of(kept, request, key_tokens // TILE, head_step, h, p)
            far_part = pick(dot(halves_t(far_tiles(far_k, used)), far_ds[h, :, cols], NN))
            dq[cols, lanes(h)] = (dq_t[:, cols] + far_part).astype(jnp.bfloat16).T
    stores.append(pltpu.make_async_copy(dq, dq_out, out_sems.at[heads, 0]))
    stores[-1].start()
    each(slots, lambda s: keep(s).wait())
    for copy in stores:
        copy.wait()


def finish_kernel(head_step, wanted, back_in, tiles, dk_in, dv_in, dk, dv, back, acc, out_k, out_v, sems):
    del dk_in, dv_in
    slots = back.shape[0] * CAP
    fetches = [
        pltpu.make_async_copy(back_in, back, sems.at[2, 0]),
        pltpu.make_async_copy(tiles, acc, sems.at[2, 1]),
    ]
    for fetch in fetches:
        fetch.start()

    def code_of(s):
        return wanted[s // CAP, s % CAP]

    def first_slot(s):
        code = code_of(s)
        if isinstance(s, int):
            found = jnp.int32(s)
            for r in reversed(range(s)):
                found = jnp.where(codes[r] == code, r, found)
            return found
        return lax.fori_loop(
            0, s, lambda r, f: jnp.where(code_of(s - 1 - r) == code, s - 1 - r, f), s
        )

    codes = [code_of(s) for s in range(slots)] if slots <= 16 else None

    def copies(s):
        tile, head = pair_of(wanted, s, head_step)
        rows = pl.ds(pl.multiple_of(tile * TILE, TILE), TILE)
        cols = pl.ds(pl.multiple_of(head * HD, HD), HD)
        return (
            pltpu.make_async_copy(out_k.at[s], dk.at[rows, cols], sems.at[0, s]),
            pltpu.make_async_copy(out_v.at[s], dv.at[rows, cols], sems.at[1, s]),
        )

    def add(s):
        slot = firsts[s] if firsts else first_slot(s)
        acc[slot, :, :HD] += back[s // CAP, s % CAP].astype(jnp.float32)
        acc[slot, :, HD:] += back[s // CAP, CAP + s % CAP].astype(jnp.float32)

    def start(s):
        @pl.when((firsts[s] if firsts else first_slot(s)) == s)
        def _():
            out_k[s] = acc[s, :, :HD].astype(jnp.bfloat16)
            out_v[s] = acc[s, :, HD:].astype(jnp.bfloat16)
            for c in copies(s):
                c.start()

    def finish(s):
        @pl.when((firsts[s] if firsts else first_slot(s)) == s)
        def _():
            for c in copies(s):
                c.wait()

    firsts = [first_slot(s) for s in range(slots)] if slots <= 16 else None
    for fetch in fetches:
        fetch.wait()
    each(slots, add)
    each(slots, start)
    each(slots, finish)


def local(q_raw, k_raw, values, q_gain, k_gain, cotangent, kept_tiles):
    slab_count = lax.axis_size("slab")
    group_count = lax.axis_size("head")
    own_slab = lax.axis_index("slab")
    query_tiles, head_count, kept_count = kept_tiles.shape
    local_width = q_raw.shape[1]
    key_tiles = k_raw.shape[0] // TILE
    query_tokens, key_tokens = q_raw.shape[0], k_raw.shape[0]
    full_width = local_width * group_count
    head_step = pl.next_power_of_2(head_count)
    slots = slab_count * CAP
    vmem = pltpu.CompilerParams(vmem_limit_bytes=60 << 20)

    def grant(limit):
        return pltpu.CompilerParams(vmem_limit_bytes=limit)


    def array(shape, dtype=jnp.bfloat16):
        return jax.ShapeDtypeStruct(shape, dtype)

    by_head = kept_tiles.transpose(1, 0, 2)
    owner = lax.div(by_head, key_tiles)
    code = (by_head - owner * key_tiles) * head_step + lax.broadcasted_iota(
        jnp.int32, by_head.shape, 0
    )
    owner = jnp.where(lax.broadcasted_iota(jnp.int32, by_head.shape, 2) < NEAR, -1, owner)
    mine = owner[None] == jnp.arange(slab_count, dtype=jnp.int32)[:, None, None, None]
    low = jnp.max(jnp.where(mine, LIMIT - code[None], 0), axis=(1, 2, 3))
    high = jnp.max(jnp.where(mine, code[None] + 1, 0), axis=(1, 2, 3))
    lane = jnp.arange(HD, dtype=jnp.int32)[None, :]
    request = jnp.where(lane == 0, low[:, None], high[:, None])
    wanted = lax.all_to_all(
        jnp.broadcast_to(request[:, None], (slab_count, 8, HD)),
        "slab", split_axis=0, concat_axis=0, tiled=True,
    )[:, 0]
    wanted = jnp.where(wanted == 0, 0, jnp.where(lane == 0, LIMIT - wanted, wanted - 1))
    kept_flat = kept_tiles.reshape(query_tiles, head_count * kept_count)

    key_rows, query_rows = key_tokens // HD, query_tokens // HD
    stat_rows = -(-(key_rows + query_rows) // 8) * 8
    k_sum = jnp.sum(jnp.square(k_raw.astype(jnp.float32)), axis=1)
    q_sum = jnp.sum(jnp.square(q_raw.astype(jnp.float32)), axis=1)
    pad = (stat_rows - key_rows - query_rows) * HD
    stats = jnp.concatenate((k_sum, q_sum, jnp.zeros((pad,), jnp.float32))).reshape(stat_rows, HD)
    parts = [stats]
    for step in range(1, group_count):
        parts.append(
            lax.ppermute(
                stats, "head", [(i, (i + step) % group_count) for i in range(group_count)]
            )
        )

    q_row, k_row = q_gain.reshape(1, local_width), k_gain.reshape(1, local_width)
    far_shape = (slab_count, 2 * CAP, TILE, HD)
    outgoing = pl.pallas_call(
        functools.partial(gather_kernel, full_width, head_step, group_count),
        out_shape=array(far_shape),
        in_specs=[SMEM] + [VMEM] * group_count + [VMEM, HBM, HBM],
        out_specs=HBM,
        scratch_shapes=[
            pltpu.VMEM((slots, TILE, HD), jnp.bfloat16),
            pltpu.VMEM((slots, TILE, HD), jnp.bfloat16),
            pltpu.VMEM((slots, TILE, HD), jnp.bfloat16),
            pltpu.VMEM((key_tokens, HD), jnp.float32),
            pltpu.SemaphoreType.DMA((4, slots)),
        ],
        compiler_params=grant(62700000),
        name="gather_far",
    )(wanted, *parts, k_gain, k_raw, values)
    far = lax.all_to_all(outgoing, "slab", split_axis=0, concat_axis=0, tiled=True)

    near = kept_tiles[:, :, :NEAR] - own_slab * key_tiles
    tile_ids = jnp.arange(key_tiles, dtype=jnp.int32)
    kept = jnp.any(near[:, :, :, None] == tile_ids, axis=2)
    mask = jnp.where(kept, 0.0, MASKED).astype(jnp.float32).transpose(1, 2, 0)
    mask = jnp.repeat(mask, TILE, axis=2)

    def column(tokens):
        return pl.BlockSpec((tokens, HD), lambda h: (0, h))

    def each_head(*shape):
        return pl.BlockSpec((1, *shape), lambda h: (h,) + (0,) * len(shape))

    all_stats = pl.BlockSpec((stat_rows, HD), lambda h: (0, 0))
    gain_spec = pl.BlockSpec((1, HD), lambda h: (0, h))
    queries, keys = (query_tokens, local_width), (key_tokens, local_width)
    keys_t, queries_t = (head_count, HD, key_tokens), (head_count, HD, query_tokens)
    stat_shape = (head_count, 8, query_tokens)
    probs_shape = (head_count, key_tokens, query_tokens)
    far_ds_shape = (head_count, 2 * TILE, query_tokens)
    far_k_shape = (slab_count, CAP, TILE, HD)
    kn, qn, kn_t, v_t, cot_t, stat = pl.pallas_call(
        functools.partial(near_kernel, full_width, group_count),
        grid=(head_count,),
        in_specs=[all_stats] * group_count
        + [
            column(query_tokens),
            column(key_tokens),
            column(key_tokens),
            column(query_tokens),
            gain_spec,
            gain_spec,
            each_head(key_tiles, query_tokens),
        ],
        out_specs=[
            column(key_tokens),
            column(query_tokens),
            each_head(HD, key_tokens),
            each_head(HD, key_tokens),
            each_head(HD, query_tokens),
            each_head(8, query_tokens),
        ],
        out_shape=[
            array(keys),
            array(queries),
            array(keys_t),
            array(keys_t),
            array(queries_t),
            array(stat_shape, jnp.float32),
        ],
        scratch_shapes=[pltpu.VMEM((key_tokens, query_tokens), jnp.float32)],
        compiler_params=pltpu.CompilerParams(vmem_limit_bytes=60 << 20),
        name="near",
    )(*parts, q_raw, k_raw, values, cotangent, q_row, k_row, mask)

    attn_out, probs, delta, far_ds, far_k, far_grad = pl.pallas_call(
        functools.partial(meet_kernel, head_step),
        in_specs=[SMEM] * 2 + [HBM] * 8,
        out_specs=[HBM] * 6,
        out_shape=[
            array(queries),
            array(probs_shape),
            array(stat_shape, jnp.float32),
            array(far_ds_shape),
            array(far_k_shape),
            array(far_shape),
        ],
        scratch_shapes=[
            pltpu.VMEM(far_shape, jnp.bfloat16),
            pltpu.VMEM(keys, jnp.bfloat16),
            pltpu.VMEM(queries, jnp.bfloat16),
            pltpu.VMEM(stat_shape, jnp.float32),
            pltpu.VMEM((head_count, key_tiles, query_tokens), jnp.float32),
            pltpu.VMEM(keys_t, jnp.bfloat16),
            pltpu.VMEM(queries_t, jnp.bfloat16),
            pltpu.VMEM(queries, jnp.bfloat16),
            pltpu.VMEM(queries, jnp.bfloat16),
            pltpu.VMEM(probs_shape, jnp.bfloat16),
            pltpu.VMEM(stat_shape, jnp.float32),
            pltpu.VMEM(far_ds_shape, jnp.bfloat16),
            pltpu.VMEM(far_ds_shape, jnp.bfloat16),
            pltpu.VMEM(queries_t, jnp.float32),
            pltpu.VMEM(stat_shape, jnp.float32),
            pltpu.VMEM((slots, TILE, HD), jnp.float32),
            pltpu.VMEM((slots, TILE, HD), jnp.float32),
            pltpu.VMEM(far_shape, jnp.bfloat16),
            pltpu.SemaphoreType.DMA((head_count + 1, 7)),
            pltpu.SemaphoreType.DMA((head_count + 5,)),
        ],
        compiler_params=vmem,
        name="meet",
    )(kept_flat, request, kn, qn, stat, mask, v_t, cot_t, cotangent, far)
    back = lax.all_to_all(far_grad, "slab", split_axis=0, concat_axis=0, tiled=True)

    dq_normed, dk, dv, tiles = pl.pallas_call(
        functools.partial(grad_kernel, head_step),
        in_specs=[SMEM] * 3 + [HBM] * 8,
        out_specs=[HBM] * 4,
        out_shape=[
            array(queries),
            array(keys),
            array(keys),
            array((slots, TILE, 2 * HD), jnp.float32),
        ],
        scratch_shapes=[
            pltpu.VMEM(keys_t, jnp.bfloat16),
            pltpu.VMEM(queries, jnp.bfloat16),
            pltpu.VMEM(keys, jnp.bfloat16),
            pltpu.VMEM(queries, jnp.bfloat16),
            pltpu.VMEM((head_count, key_tokens, 2 * query_tokens), jnp.bfloat16),
            pltpu.VMEM(stat_shape, jnp.float32),
            pltpu.VMEM(far_ds_shape, jnp.bfloat16),
            pltpu.VMEM(far_k_shape, jnp.bfloat16),
            pltpu.VMEM((2, 2 * query_tokens, 2 * HD), jnp.bfloat16),
            pltpu.VMEM((head_count, key_tokens, 2 * HD), jnp.float32),
            pltpu.VMEM(queries, jnp.bfloat16),
            pltpu.VMEM(keys, jnp.bfloat16),
            pltpu.VMEM(keys, jnp.bfloat16),
            pltpu.SemaphoreType.DMA((head_count + 1, 7)),
            pltpu.SemaphoreType.DMA((head_count + 1, 2)),
            pltpu.SemaphoreType.DMA((slots,)),
        ],
        compiler_params=vmem,
        name="grad",
    )(kept_flat, request, wanted, kn_t, qn, values, cotangent, probs, delta, far_ds, far_k)

    dk, dv = pl.pallas_call(
        functools.partial(finish_kernel, head_step),
        out_shape=[array(keys), array(keys)],
        in_specs=[SMEM, ANYWHERE, HBM, HBM, HBM],
        out_specs=[HBM, HBM],
        scratch_shapes=[
            pltpu.VMEM(far_shape, jnp.bfloat16),
            pltpu.VMEM((slots, TILE, 2 * HD), jnp.float32),
            pltpu.VMEM((slots, TILE, HD), jnp.bfloat16),
            pltpu.VMEM((slots, TILE, HD), jnp.bfloat16),
            pltpu.SemaphoreType.DMA((3, slots)),
        ],
        input_output_aliases={3: 0, 4: 1},
        compiler_params=grant(50 << 20),
        name="finish",
    )(wanted, back, tiles, dk, dv)
    return attn_out, dq_normed, dk, dv


def solution(mesh):
    tokens = P("slab", "head")
    return jax.shard_map(
        local,
        mesh=mesh,
        in_specs=(tokens, tokens, tokens, P("head"), P("head"), tokens, P("slab", "head", None)),
        out_specs=(tokens, tokens, tokens, tokens),
        check_vma=False,
    )
```

time: 80.2 us -> 76.2 us (0.950)
  Pallas kernels: 43.4 us -> 38.6 us
  starting transfers between devices: 17.4 us -> 19.2 us
  waiting for transfers between devices: 6.69 us -> 5.07 us
    all_to_all x1, waiting for transfers between devices: 5.19 us -> 1.66 us  [local(): lax.all_to_all(jnp.broadcast_to(request[:, None], (slab_count, 8, HD)), '...]
    pallas_call x3, Pallas kernels: 29.8 us -> 26.7 us  [the longest x1 12.5 us: local(): pl.pallas_call(functools.partial(meet_kernel, head_step), in_specs=[SMEM]...]
    all_to_all x1, starting transfers between devices: 3.51 us -> 5.76 us  [local(): lax.all_to_all(outgoing, 'slab', split_axis=0, concat_axis=0, tiled=True)]
    pallas_call x1, Pallas kernels: 10.5 us -> 8.85 us  [local(): pl.pallas_call(functools.partial(near_kernel, full_width, group_count), g...]
    ppermute x3, starting transfers between devices: 3.23 us -> 1.79 us  [local(): lax.ppermute(stats, 'head', [(i, (i + step) % group_count) for i in range...]
    all_to_all x1, starting transfers between devices: 5.84 us -> 7.28 us  [local(): lax.all_to_all(jnp.broadcast_to(request[:, None], (slab_count, 8, HD)), '...]
    gather x2 -> x0, local copies, waits for them, and re-layouts: 0.87 us -> none  [local(): use_slot = far_owner * CAP + (code != low[far_owner]).astype(jnp.int32)]
    unnamed x20 -> x23, local copies, waits for them, and re-layouts: 2.23 us -> 2.95 us
  transfers between devices with their start and end apart: 6 -> 6, of which waited for: 3 -> 5; matrix products, arithmetic and copies ran while one was open for 7% -> 9% of each run, Pallas kernels for 31% -> 28%
where the time goes in v3:
time: 76.2 us; the launch traced here: 75.4 us
  Pallas kernels  38.6 us (51%)
  starting transfers between devices  19.2 us (25%)
  local copies, waits for them, and re-layouts  6.63 us (9%)
  waiting for transfers between devices  5.07 us (7%)
  other arithmetic  4.95 us (6%)
  between operations  0.94 us (1%)
    pallas_call x1, Pallas kernels, local(): pl.pallas_call(functools.partial(meet_kernel, head_step), in_specs=[SMEM]...  12.5 us
    pallas_call x1, Pallas kernels, local(): pl.pallas_call(functools.partial(grad_kernel, head_step), in_specs=[SMEM]...  12.1 us
    pallas_call x1, Pallas kernels, local(): pl.pallas_call(functools.partial(near_kernel, full_width, group_count), g...  8.85 us
    all_to_all x1, starting transfers between devices, local(): lax.all_to_all(jnp.broadcast_to(request[:, None], (slab_count, 8, HD)), '...  7.28 us
    all_to_all x1, starting transfers between devices, local(): lax.all_to_all(outgoing, 'slab', split_axis=0, concat_axis=0, tiled=True)  5.76 us
    all_to_all x1, starting transfers between devices, local(): lax.all_to_all(far_grad, 'slab', split_axis=0, concat_axis=0, tiled=True)  4.33 us
    pallas_call x1, Pallas kernels, local(): pl.pallas_call(functools.partial(gather_kernel, full_width, head_step, gr...  3.12 us
    unnamed x23, local copies, waits for them, and re-layouts  2.95 us
  transfers between devices with their start and end apart: 6, of which 5 were waited for; matrix products, arithmetic and copies ran while one was open for 9% of the time, Pallas kernels for 28%

profile of v3, /device:TPU:0, one launch (start us, length us, event | category | flops | bytes accessed | tf_op | source)
XLA Modules:
  0.0 75.4 jit_solution(7453209529668407941)
XLA Ops:
  0.7 0.7 broadcast_add_fusion
  1.4 0.2 select_reduce_fusion.1
  1.7 0.6 broadcast_in_dim.96
  2.3 7.3 %all-to-all-start = ((s32[8,8,128]{2,1,0:T(8,128)}), s32[8,8,128]{2,1,0:T(8,128)S(1)}, u32[]{:S(2)}, u32[]{:S(2)}) async-start(s32[8,8,128]{2,1,0:T(8,128)} %broadcast_in_dim.96), calls=%async_computation | async-start | bytes 65536 | tf_op jit(solution)/shard_map/all_to_all | solution.py:494
  9.6 1.2 %multiply_reduce_fusion.1 = f32[384]{0:T(512)S(1)} fusion(bf16[384,640]{1,0:T(8,128)(2,1)} %refs_4_.2), kind=kLoop, calls=%fused_computation.1 | loop fusion | flops 736896 | bytes 493056 | tf_op jit(solution)/shard_map/reduce_sum | solution.py:504
  10.8 2.0 %multiply_reduce_fusion = f32[1536]{0:T(1024)S(1)} fusion(bf16[1536,640]{1,0:T(8,128)(2,1)} %refs_5_.3), kind=kLoop, calls=%fused_computation | loop fusion | flops 2947584 | bytes 1972224 | tf_op jit(solution)/shard_map/reduce_sum | solution.py:503
  12.8 0.7 collective-permute-start.2
  13.5 0.9 %collective-permute-start.1 = (f32[16,128]{1,0:T(8,128)S(1)}, f32[16,128]{1,0:T(8,128)S(1)}, u32[]{:S(2)}, u32[]{:S(2)}) collective-permute-start(f32[16,128]{1,0:T(8,128)S(1)} %maximum_bitcast_fusion.refs_0_), channel_id=1, source_target_pairs={{0,2},{1,3},{2,0},{3,1},{4,6},{5,7},{6,4},{7,5},{8,10},{9,11},{10,... | collective-permute-start | bytes 24584 | tf_op jit(solution)/shard_map/ppermute | solution.py:510
  14.4 0.2 collective-permute-start
  14.6 1.7 %all-to-all-done = s32[8,8,128]{2,1,0:T(8,128)S(1)} async-done(((s32[8,8,128]{2,1,0:T(8,128)}), s32[8,8,128]{2,1,0:T(8,128)S(1)}, u32[]{:S(2)}, u32[]{:S(2)}) %all-to-all-start) | async-done | bytes 32800 | tf_op jit(solution)/shard_map/all_to_all | solution.py:494
  16.3 0.6 fusion.4.wanted
  16.9 0.3 collective-permute-done.1.refs_2_
  17.2 0.3 collective-permute-done.refs_1_
  17.5 0.2 copy-done.7
  17.8 0.6 copy-done.8
  18.4 3.1 %gather_far.1 = bf16[8,4,64,128]{3,2,1,0:T(8,128)(2,1)} custom-call(s32[8,128]{1,0:T(8,128)} %fusion.4.wanted, f32[16,128]{1,0:T(8,128)} %copy-done.4, f32[16,128]{1,0:T(8,128)} %copy-done.8, f32[16,128]{1,0:T(8,128)} %copy-done.7, f32[16,128]{1,0:T(8,128)} %copy-done.6, f32[640]{0:T(1024)} %refs_4_.3, bf16[1536,640]{1,0:T(8,128)(2,1)} %refs_5_.3, ...), custom_call_target="tpu_custom_call" | custom-call | tf_op jit(solution)/shard_map/gather_far/pallas_call | solution.py:517
  21.5 5.8 %all-to-all-start.1 = ((bf16[8,4,64,128]{3,2,1,0:T(8,128)(2,1)}), bf16[8,4,64,128]{3,2,1,0:T(8,128)(2,1)S(1)}, u32[]{:S(2)}, u32[]{:S(2)}) async-start(bf16[8,4,64,128]{3,2,1,0:T(8,128)(2,1)} %gather_far.1), calls=%async_computation.1 | async-start | bytes 1048576 | tf_op jit(solution)/shard_map/all_to_all | solution.py:532
  27.3 0.6 reshape.75.refs_9_
  27.9 0.6 reshape.74.refs_8_
  28.5 0.1 copy.21
  28.6 0.7 reshape.72.kept
  29.5 0.2 broadcast_in_dim.95
  29.7 0.8 %reshape.76.refs_10_.mask_in = f32[5,24,384]{2,1,0:T(8,128)} reshape(f32[5,24,6,64]{3,2,1,0:T(8,128)S(1)} %broadcast_in_dim.95) | data formatting | bytes 368640 | tf_op jit(solution)/shard_map/reshape | solution.py:538
  30.5 8.8 %near.1 = (bf16[1536,640]{1,0:T(8,128)(2,1)}, bf16[384,640]{1,0:T(8,128)(2,1)}, bf16[5,128,1536]{2,1,0:T(8,128)(2,1)}, bf16[5,128,1536]{2,1,0:T(8,128)(2,1)}, bf...) custom-call(f32[16,128]{1,0:T(8,128)} %copy-done.4, f32[16,128]{1,0:T(8,128)} %copy-done.8, f32[16,128]{1,0:T(8,128)} %copy-done.7, ...), custom_call_target="tpu_custom_call" | custom-call | tf_op jit(solution)/shard_map/near/pallas_call | solution.py:554
  39.3 1.7 %all-to-all-done.1.far_in = bf16[8,4,64,128]{3,2,1,0:T(8,128)(2,1)S(1)} async-done(((bf16[8,4,64,128]{3,2,1,0:T(8,128)(2,1)}), bf16[8,4,64,128]{3,2,1,0:T(8,128)(2,1)S(1)}, u32[]{:S(2)}, u32[]{:S(2)}) %all-to-all-start.1) | async-done | bytes 524320 | tf_op jit(solution)/shard_map/all_to_all | solution.py:532
  41.0 0.8 %copy-done.2 = bf16[8,4,64,128]{3,2,1,0:T(8,128)(2,1)} copy-done((bf16[8,4,64,128]{3,2,1,0:T(8,128)(2,1)}, bf16[8,4,64,128]{3,2,1,0:T(8,128)(2,1)S(1)}, u32[]{:S(2)}) %copy-start.2) | copy-done | bytes 524312
  41.9 12.5 %meet.1 = (bf16[384,640]{1,0:T(8,128)(2,1)}, bf16[5,1536,384]{2,1,0:T(8,128)(2,1)}, f32[5,8,384]{2,1,0:T(8,128)}, bf16[5,128,384]{2,1,0:T(8,128)(2,1)}, bf16[8,2...) custom-call(s32[6,60]{1,0:T(8,128)} %reshape.72.kept, s32[8,128]{1,0:T(8,128)} %copy-done.5, ...), custom_call_target="tpu_custom_call" | custom-call | tf_op jit(solution)/shard_map/meet/pallas_call | solution.py:588
  54.4 4.3 %all-to-all-start.2 = ((bf16[8,4,64,128]{3,2,1,0:T(8,128)(2,1)}), bf16[8,4,64,128]{3,2,1,0:T(8,128)(2,1)S(1)}, u32[]{:S(2)}, u32[]{:S(2)}) async-start(bf16[8,4,64,128]{3,2,1,0:T(8,128)(2,1)} %get-tuple-element.34), calls=%async_computation.2 | async-start | bytes 1048576 | tf_op jit(solution)/shard_map/all_to_all | solution.py:625
  58.7 12.1 %grad.1 = (bf16[384,640]{1,0:T(8,128)(2,1)}, bf16[1536,640]{1,0:T(8,128)(2,1)}, bf16[1536,640]{1,0:T(8,128)(2,1)}, f32[16,64,256]{2,1,0:T(8,128)}) custom-call(s32[6,60]{1,0:T(8,128)} %reshape.72.kept, s32[8,128]{1,0:T(8,128)} %copy-done.5, s32[8,128]{1,0:T(8,128)} %fusion.4.wanted, bf16[5,128,1536]{2,1,0:T(8,128)(2,1)} %get-tuple-element.28.kn_t_in, ...), custom_call_target="tpu_custom_call" | custom-call | tf_op jit(solution)/shard_map/grad/pallas_call | solution.py:627
  70.8 1.1 %all-to-all-done.2.back_in = bf16[8,4,64,128]{3,2,1,0:T(8,128)(2,1)S(1)} async-done(((bf16[8,4,64,128]{3,2,1,0:T(8,128)(2,1)}), bf16[8,4,64,128]{3,2,1,0:T(8,128)(2,1)S(1)}, u32[]{:S(2)}, u32[]{:S(2)}) %all-to-all-start.2) | async-done | bytes 524320 | tf_op jit(solution)/shard_map/all_to_all | solution.py:625
  71.9 1.2 %copy-done = f32[16,64,256]{2,1,0:T(8,128)S(1)} copy-done((f32[16,64,256]{2,1,0:T(8,128)S(1)}, f32[16,64,256]{2,1,0:T(8,128)}, u32[]{:S(2)}) %copy-start) | copy-done | bytes 1048600
  73.1 2.1 %finish.1 = (bf16[1536,640]{1,0:T(8,128)(2,1)}, bf16[1536,640]{1,0:T(8,128)(2,1)}) custom-call(s32[8,128]{1,0:T(8,128)S(1)} %copy-done.1, bf16[8,4,64,128]{3,2,1,0:T(8,128)(2,1)S(1)} %all-to-all-done.2.back_in, f32[16,64,256]{2,1,0:T(8,128)S(1)} %copy-done, bf16[1536,640]{1,0:T(8,128)(2,1)} %get-tuple-element.36.dk_in, ...), custom_call_target="tpu_custom_call", output_to_operand_aliasing={{0}: (3, {}), {1}: (4, {})} | custom-call | tf_op jit(solution)/shard_map/finish/pallas_call | solution.py:659
  (30 shorter events, 0.4 us)
Async XLA Ops:
  1.7 19.8 %copy-start.5 = (s32[8,128]{1,0:T(8,128)}, s32[8,128]{1,0:T(8,128)S(1)}, u32[]{:S(2)}) copy-start(s32[8,128]{1,0:T(8,128)S(1)} %broadcast_select_fusion.request) | copy-start | bytes 12292
  2.3 14.0 %all-to-all-start = ((s32[8,8,128]{2,1,0:T(8,128)}), s32[8,8,128]{2,1,0:T(8,128)S(1)}, u32[]{:S(2)}, u32[]{:S(2)}) async-start(s32[8,8,128]{2,1,0:T(8,128)} %broadcast_in_dim.96), calls=%async_computation | async-start | bytes 65536 | tf_op jit(solution)/shard_map/all_to_all | solution.py:494
  12.8 4.7 %copy-start.4 = (f32[16,128]{1,0:T(8,128)}, f32[16,128]{1,0:T(8,128)S(1)}, u32[]{:S(2)}) copy-start(f32[16,128]{1,0:T(8,128)S(1)} %maximum_bitcast_fusion.refs_0_) | copy-start | bytes 24580
  12.8 4.1 %collective-permute-start.2 = (f32[16,128]{1,0:T(8,128)S(1)}, f32[16,128]{1,0:T(8,128)S(1)}, u32[]{:S(2)}, u32[]{:S(2)}) collective-permute-start(f32[16,128]{1,0:T(8,128)S(1)} %maximum_bitcast_fusion.refs_0_), channel_id=1, source_target_pairs={{0,3},{1,0},{2,1},{3,2},{4,7},{5,4},{6,5},{7,6},{8,11},{9,8},{10,9... | collective-permute-start | bytes 24584 | tf_op jit(solution)/shard_map/ppermute | solution.py:510
  13.5 3.7 %collective-permute-start.1 = (f32[16,128]{1,0:T(8,128)S(1)}, f32[16,128]{1,0:T(8,128)S(1)}, u32[]{:S(2)}, u32[]{:S(2)}) collective-permute-start(f32[16,128]{1,0:T(8,128)S(1)} %maximum_bitcast_fusion.refs_0_), channel_id=1, source_target_pairs={{0,2},{1,3},{2,0},{3,1},{4,6},{5,7},{6,4},{7,5},{8,10},{9,11},{10,... | collective-permute-start | bytes 24584 | tf_op jit(solution)/shard_map/ppermute | solution.py:510
  14.4 3.1 %collective-permute-start = (f32[16,128]{1,0:T(8,128)S(1)}, f32[16,128]{1,0:T(8,128)S(1)}, u32[]{:S(2)}, u32[]{:S(2)}) collective-permute-start(f32[16,128]{1,0:T(8,128)S(1)} %maximum_bitcast_fusion.refs_0_), channel_id=1, source_target_pairs={{0,1},{1,2},{2,3},{3,0},{4,5},{5,6},{6,7},{7,4},{8,9},{9,10},{10,1... | collective-permute-start | bytes 24584 | tf_op jit(solution)/shard_map/ppermute | solution.py:510
  16.9 10.4 %copy-start.9 = (f32[640]{0:T(1024)S(1)}, f32[640]{0:T(1024)}, u32[]{:S(2)}) copy-start(f32[640]{0:T(1024)} %refs_4_.3) | copy-start | bytes 7684
  16.9 11.0 %copy-start.3 = (s32[6,5,12]{2,0,1:T(8,128)S(1)}, s32[6,5,12]{2,0,1:T(8,128)}, u32[]{:S(2)}) copy-start(s32[6,5,12]{2,0,1:T(8,128)} %param.13) | copy-start | bytes 4324
  16.9 11.0 %copy-start.10 = (f32[640]{0:T(1024)S(1)}, f32[640]{0:T(1024)}, u32[]{:S(2)}) copy-start(f32[640]{0:T(1024)} %param.10) | copy-start | bytes 7684
  16.9 0.6 copy-start.6
  17.2 0.6 copy-start.7
  17.8 0.6 copy-start.8
  21.5 19.5 %all-to-all-start.1 = ((bf16[8,4,64,128]{3,2,1,0:T(8,128)(2,1)}), bf16[8,4,64,128]{3,2,1,0:T(8,128)(2,1)S(1)}, u32[]{:S(2)}, u32[]{:S(2)}) async-start(bf16[8,4,64,128]{3,2,1,0:T(8,128)(2,1)} %gather_far.1), calls=%async_computation.1 | async-start | bytes 1048576 | tf_op jit(solution)/shard_map/all_to_all | solution.py:532
  41.0 0.8 %copy-start.2 = (bf16[8,4,64,128]{3,2,1,0:T(8,128)(2,1)}, bf16[8,4,64,128]{3,2,1,0:T(8,128)(2,1)S(1)}, u32[]{:S(2)}) copy-start(bf16[8,4,64,128]{3,2,1,0:T(8,128)(2,1)S(1)} %all-to-all-done.1.far_in) | copy-start | bytes 1572868
  54.4 17.5 %all-to-all-start.2 = ((bf16[8,4,64,128]{3,2,1,0:T(8,128)(2,1)}), bf16[8,4,64,128]{3,2,1,0:T(8,128)(2,1)S(1)}, u32[]{:S(2)}, u32[]{:S(2)}) async-start(bf16[8,4,64,128]{3,2,1,0:T(8,128)(2,1)} %get-tuple-element.34), calls=%async_computation.2 | async-start | bytes 1048576 | tf_op jit(solution)/shard_map/all_to_all | solution.py:625
  58.7 13.2 %copy-start.1 = (s32[8,128]{1,0:T(8,128)S(1)}, s32[8,128]{1,0:T(8,128)}, u32[]{:S(2)}) copy-start(s32[8,128]{1,0:T(8,128)} %fusion.4.wanted) | copy-start | bytes 12292
  71.9 1.2 %copy-start = (f32[16,64,256]{2,1,0:T(8,128)S(1)}, f32[16,64,256]{2,1,0:T(8,128)}, u32[]{:S(2)}) copy-start(f32[16,64,256]{2,1,0:T(8,128)} %get-tuple-element.35.tiles) | copy-start | bytes 3145732

commit v4 on v3

--- a/solution.py
+++ b/solution.py
@@ -181,6 +181,14 @@
     cot_t[0] = cot[...].T
 
 
+def loop(count, body):
+    lax.fori_loop(0, count, lambda i, carry: (body(i), carry)[1], 0)
+
+
+def lanes(h):
+    return pl.ds(pl.multiple_of(h * HD, HD), HD)
+
+
 def meet_kernel(head_step, kept, request, kn_in, qn_in, stat_in, mask_in, v_t_in, cot_t_in, cot_in,
                 far_in, attn_out, probs_out, delta_out, far_ds_out, far_k_out, far_grad_out,
                 far, kn, qn, stat, mask, v_t, cot_t, cot, attn, probs, delta, far_ds, far_p, outs,
@@ -191,46 +199,48 @@
     exponent = score_scale * LOG2E
     slots = far.shape[0] * CAP
 
-    def lanes(h):
-        return slice(h * HD, (h + 1) * HD)
-
-    fetches = [
-        [
+    def fetches(h):
+        return [
             pltpu.make_async_copy(src, dst, in_sems.at[h, n])
             for n, (src, dst) in enumerate(
                 (
-                    (qn_in.at[:, lanes(h)], qn.at[:, lanes(h)]),
+                    (qn_in.at[:, lanes(h)], qn.at[h]),
                     (stat_in.at[h], stat.at[h]),
                     (mask_in.at[h], mask.at[h]),
-                    (kn_in.at[:, lanes(h)], kn.at[:, lanes(h)]),
+                    (kn_in.at[:, lanes(h)], kn.at[h]),
                     (v_t_in.at[h], v_t.at[h]),
                     (cot_t_in.at[h], cot_t.at[h]),
-                    (cot_in.at[:, lanes(h)], cot.at[:, lanes(h)]),
+                    (cot_in.at[:, lanes(h)], cot.at[h]),
                 )
             )
         ]
-        for h in range(heads)
-    ]
+
     fetch_far = pltpu.make_async_copy(far_in, far, in_sems.at[heads, 0])
+    far_store = pltpu.make_async_copy(far.at[:, :CAP], far_k_out, out_sems.at[heads, 0])
+
+    def head_stores(h):
+        return (
+            pltpu.make_async_copy(probs.at[h], probs_out.at[h], out_sems.at[h, 0]),
+            pltpu.make_async_copy(attn.at[h], attn_out.at[:, lanes(h)], out_sems.at[h, 1]),
+        )
+
     fetch_far.start()
-    for first, last in ((0, 2), (2, 5), (5, 7)):
-        for h in range(heads):
-            for copy in fetches[h][first:last]:
-                copy.start()
-    stores = []
+    loop(heads, lambda h: [copy.start() for copy in fetches(h)[:2]])
+    loop(heads, lambda h: [copy.start() for copy in fetches(h)[2:]])
     k_acc[...] = jnp.zeros_like(k_acc)
     v_acc[...] = jnp.zeros_like(v_acc)
-    used = [
-        [slots_of(kept, request, key_tiles, head_step, h, p) for p in range(pairs)]
-        for h in range(heads)
-    ]
+    fetch_far.wait()
+    far_store.start()
+
+    def used(h, p):
+        return slots_of(kept, request, key_tiles, head_step, h, p)
 
     def far_scores(h):
-        for copy in fetches[h][:2]:
+        for copy in fetches(h)[:2]:
             copy.wait()
         for p in range(pairs):
             cols = slice(p * HD, (p + 1) * HD)
-            far_s = pick(dot(far_tiles(far, used[h][p]), qn[cols, lanes(h)], NT)) * exponent
+            far_s = pick(dot(far_tiles(far, used(h, p)), qn[h, cols, :], NT)) * exponent
             near_top = stat[h, 0:1, cols]
             top = jnp.maximum(near_top, jnp.max(far_s, axis=0, keepdims=True))
             total = stat[h, 1:2, cols] * jnp.exp2(near_top - top) + jnp.sum(
@@ -243,70 +253,65 @@
     step = 4 * TILE
 
     def near_part(h):
-        for copy in fetches[h][2:5]:
+        for copy in fetches(h)[2:]:
             copy.wait()
-        for c in range(0, key_tiles * TILE, step):
-            block = dot(kn[c : c + step, lanes(h)], qn[:, lanes(h)], NT) * exponent
+
+        for first in range(0, key_tiles * TILE, step):
+            block = dot(kn[h, first : first + step, :], qn[h], NT) * exponent
             for t in range(step // TILE):
-                row = mask[h, c // TILE + t, :][None] - logs[h, 0:1, :]
-                probs[h, c + t * TILE : c + (t + 1) * TILE, :] = jnp.exp2(
+                row = mask[h, first // TILE + t, :][None] - logs[h, 0:1, :]
+                probs[h, first + t * TILE : first + (t + 1) * TILE, :] = jnp.exp2(
                     block[t * TILE : (t + 1) * TILE] + row
                 ).astype(jnp.bfloat16)
-        outs[h] = dot(v_t[h], probs[h], NN)
-        stores.append(pltpu.make_async_copy(probs.at[h], probs_out.at[h], out_sems.at[h]))
-        stores[-1].start()
-
-    def far_part(h):
-        for copy in fetches[h][5:]:
-            copy.wait()
+
+        head_stores(h)[0].start()
+        outs[...] = dot(v_t[h], probs[h], NN)
         for p in range(pairs):
             cols = slice(p * HD, (p + 1) * HD)
-            values = far_tiles(far, used[h][p], CAP)
+            slot = used(h, p)
+            values = far_tiles(far, slot, CAP)
             weights = far_p[h, :, cols]
-            out_b = (outs[h, :, cols] + pick(dot(halves_t(values), weights, NN))).astype(
+            out_b = (outs[:, cols] + pick(dot(halves_t(values), weights, NN))).astype(
                 jnp.bfloat16
             )
-            attn[cols, lanes(h)] = out_b.T
+            attn[h, cols, :] = out_b.T
             row_delta = jnp.sum(
                 cot_t[h, :, cols].astype(jnp.float32) * out_b.astype(jnp.float32),
                 axis=0, keepdims=True,
             )
             delta[h, 0:1, cols] = row_delta
-            grad_p = pick(dot(values, cot[cols, lanes(h)], NT))
+            grad_p = pick(dot(values, cot[h, cols, :], NT))
             ds = (weights.astype(jnp.float32) * (grad_p - row_delta) * score_scale).astype(
                 jnp.bfloat16
             )
             far_ds[h, :, cols] = ds
-            grad_k = dot(ds, split_rows(qn[cols, lanes(h)]), NN)
-            grad_v = dot(weights, split_rows(cot[cols, lanes(h)]), NN)
-            for n, s in enumerate(used[h][p]):
+            grad_k = dot(ds, split_rows(qn[h, cols, :]), NN)
+            grad_v = dot(weights, split_rows(cot[h, cols, :]), NN)
+            for n, s in enumerate(slot):
                 rows = slice(n % CAP * TILE, (n % CAP + 1) * TILE)
                 half = slice(n // CAP * HD, (n // CAP + 1) * HD)
                 k_acc[s] += grad_k[rows, half]
                 v_acc[s] += grad_v[rows, half]
-
-    fetch_far.wait()
-    stores.append(pltpu.make_async_copy(far.at[:, :CAP], far_k_out, out_sems.at[heads]))
-    stores[-1].start()
-    for h in range(heads):
-        far_scores(h)
-    near_part(0)
-    for h in range(1, heads):
-        near_part(h)
-        far_part(h - 1)
-    far_part(heads - 1)
+        head_stores(h)[1].start()
+
+    each(heads, far_scores)
+    loop(heads, near_part)
 
     def send(s):
         far_grad[s // CAP, s % CAP] = k_acc[s].astype(jnp.bfloat16)
         far_grad[s // CAP, CAP + s % CAP] = v_acc[s].astype(jnp.bfloat16)
 
     each(slots, send)
-    for n, (src, dst) in enumerate(
-        ((far_grad, far_grad_out), (attn, attn_out), (delta, delta_out), (far_ds, far_ds_out))
-    ):
-        stores.append(pltpu.make_async_copy(src, dst, out_sems.at[heads + 1 + n]))
-        stores[-1].start()
+    stores = [
+        pltpu.make_async_copy(src, dst, out_sems.at[heads, 1 + n])
+        for n, (src, dst) in enumerate(
+            ((far_grad, far_grad_out), (delta, delta_out), (far_ds, far_ds_out))
+        )
+    ]
     for copy in stores:
+        copy.start()
+    loop(heads, lambda h: [copy.wait() for copy in head_stores(h)])
+    for copy in [far_store, *stores]:
         copy.wait()
 
 
@@ -546,6 +551,7 @@
     all_stats = pl.BlockSpec((stat_rows, HD), lambda h: (0, 0))
     gain_spec = pl.BlockSpec((1, HD), lambda h: (0, h))
     queries, keys = (query_tokens, local_width), (key_tokens, local_width)
+    keys_h, queries_h = (head_count, key_tokens, HD), (head_count, query_tokens, HD)
     keys_t, queries_t = (head_count, HD, key_tokens), (head_count, HD, query_tokens)
     stat_shape = (head_count, 8, query_tokens)
     probs_shape = (head_count, key_tokens, query_tokens)
@@ -599,25 +605,25 @@
         ],
         scratch_shapes=[
             pltpu.VMEM(far_shape, jnp.bfloat16),
-            pltpu.VMEM(keys, jnp.bfloat16),
-            pltpu.VMEM(queries, jnp.bfloat16),
+            pltpu.VMEM(keys_h, jnp.bfloat16),
+            pltpu.VMEM(queries_h, jnp.bfloat16),
             pltpu.VMEM(stat_shape, jnp.float32),
             pltpu.VMEM((head_count, key_tiles, query_tokens), jnp.float32),
             pltpu.VMEM(keys_t, jnp.bfloat16),
             pltpu.VMEM(queries_t, jnp.bfloat16),
-            pltpu.VMEM(queries, jnp.bfloat16),
-            pltpu.VMEM(queries, jnp.bfloat16),
+            pltpu.VMEM(queries_h, jnp.bfloat16),
+            pltpu.VMEM(queries_h, jnp.bfloat16),
             pltpu.VMEM(probs_shape, jnp.bfloat16),
             pltpu.VMEM(stat_shape, jnp.float32),
             pltpu.VMEM(far_ds_shape, jnp.bfloat16),
             pltpu.VMEM(far_ds_shape, jnp.bfloat16),
-            pltpu.VMEM(queries_t, jnp.float32),
+            pltpu.VMEM((HD, query_tokens), jnp.float32),
             pltpu.VMEM(stat_shape, jnp.float32),
             pltpu.VMEM((slots, TILE, HD), jnp.float32),
             pltpu.VMEM((slots, TILE, HD), jnp.float32),
             pltpu.VMEM(far_shape, jnp.bfloat16),
             pltpu.SemaphoreType.DMA((head_count + 1, 7)),
-            pltpu.SemaphoreType.DMA((head_count + 5,)),
+            pltpu.SemaphoreType.DMA((head_count + 1, 4)),
         ],
         compiler_params=vmem,
         name="meet",

time: 76.2 us -> 75.6 us (level)
  no operation moved by 1% of the time
where the time goes in v4:
time: 75.6 us; the launch traced here: 74.7 us
  Pallas kernels  38 us (50%)
  starting transfers between devices  19.2 us (25%)
  local copies, waits for them, and re-layouts  6.63 us (9%)
  waiting for transfers between devices  5.01 us (7%)
  other arithmetic  4.95 us (7%)
  between operations  0.94 us (1%)
    pallas_call x1, Pallas kernels, local(): pl.pallas_call(functools.partial(grad_kernel, head_step), in_specs=[SMEM]...  12.1 us
    pallas_call x1, Pallas kernels, local(): pl.pallas_call(functools.partial(meet_kernel, head_step), in_specs=[SMEM]...  11.9 us
    pallas_call x1, Pallas kernels, local(): pl.pallas_call(functools.partial(near_kernel, full_width, group_count), g...  8.84 us
    all_to_all x1, starting transfers between devices, local(): lax.all_to_all(jnp.broadcast_to(request[:, None], (slab_count, 8, HD)), '...  7.28 us
    all_to_all x1, starting transfers between devices, local(): lax.all_to_all(outgoing, 'slab', split_axis=0, concat_axis=0, tiled=True)  5.79 us
    all_to_all x1, starting transfers between devices, local(): lax.all_to_all(far_grad, 'slab', split_axis=0, concat_axis=0, tiled=True)  4.33 us
    pallas_call x1, Pallas kernels, local(): pl.pallas_call(functools.partial(gather_kernel, full_width, head_step, gr...  3.12 us
    unnamed x23, local copies, waits for them, and re-layouts  2.95 us
  transfers between devices with their start and end apart: 6, of which 5 were waited for; matrix products, arithmetic and copies ran while one was open for 9% of the time, Pallas kernels for 28%

profile of v4, /device:TPU:0, one launch (start us, length us, event | category | flops | bytes accessed | tf_op | source)
XLA Modules:
  0.0 74.7 jit_solution(15915063364717028328)
XLA Ops:
  0.7 0.7 broadcast_add_fusion
  1.4 0.2 select_reduce_fusion.1
  1.7 0.6 broadcast_in_dim.96
  2.3 7.3 %all-to-all-start = ((s32[8,8,128]{2,1,0:T(8,128)}), s32[8,8,128]{2,1,0:T(8,128)S(1)}, u32[]{:S(2)}, u32[]{:S(2)}) async-start(s32[8,8,128]{2,1,0:T(8,128)} %broadcast_in_dim.96), calls=%async_computation | async-start | bytes 65536 | tf_op jit(solution)/shard_map/all_to_all | solution.py:499
  9.6 1.2 %multiply_reduce_fusion.1 = f32[384]{0:T(512)S(1)} fusion(bf16[384,640]{1,0:T(8,128)(2,1)} %refs_4_.2), kind=kLoop, calls=%fused_computation.1 | loop fusion | flops 736896 | bytes 493056 | tf_op jit(solution)/shard_map/reduce_sum | solution.py:509
  10.8 2.0 %multiply_reduce_fusion = f32[1536]{0:T(1024)S(1)} fusion(bf16[1536,640]{1,0:T(8,128)(2,1)} %refs_5_.3), kind=kLoop, calls=%fused_computation | loop fusion | flops 2947584 | bytes 1972224 | tf_op jit(solution)/shard_map/reduce_sum | solution.py:508
  12.8 0.7 collective-permute-start.2
  13.5 0.9 %collective-permute-start.1 = (f32[16,128]{1,0:T(8,128)S(1)}, f32[16,128]{1,0:T(8,128)S(1)}, u32[]{:S(2)}, u32[]{:S(2)}) collective-permute-start(f32[16,128]{1,0:T(8,128)S(1)} %maximum_bitcast_fusion.refs_0_), channel_id=1, source_target_pairs={{0,2},{1,3},{2,0},{3,1},{4,6},{5,7},{6,4},{7,5},{8,10},{9,11},{10,... | collective-permute-start | bytes 24584 | tf_op jit(solution)/shard_map/ppermute | solution.py:515
  14.4 0.2 collective-permute-start
  14.6 1.7 %all-to-all-done = s32[8,8,128]{2,1,0:T(8,128)S(1)} async-done(((s32[8,8,128]{2,1,0:T(8,128)}), s32[8,8,128]{2,1,0:T(8,128)S(1)}, u32[]{:S(2)}, u32[]{:S(2)}) %all-to-all-start) | async-done | bytes 32800 | tf_op jit(solution)/shard_map/all_to_all | solution.py:499
  16.3 0.6 fusion.4.wanted
  16.9 0.3 collective-permute-done.1.refs_2_
  17.2 0.3 collective-permute-done.refs_1_
  17.5 0.2 copy-done.7
  17.8 0.6 copy-done.8
  18.4 3.1 %gather_far.1 = bf16[8,4,64,128]{3,2,1,0:T(8,128)(2,1)} custom-call(s32[8,128]{1,0:T(8,128)} %fusion.4.wanted, f32[16,128]{1,0:T(8,128)} %copy-done.4, f32[16,128]{1,0:T(8,128)} %copy-done.8, f32[16,128]{1,0:T(8,128)} %copy-done.7, f32[16,128]{1,0:T(8,128)} %copy-done.6, f32[640]{0:T(1024)} %refs_4_.3, bf16[1536,640]{1,0:T(8,128)(2,1)} %refs_5_.3, ...), custom_call_target="tpu_custom_call" | custom-call | tf_op jit(solution)/shard_map/gather_far/pallas_call | solution.py:522
  21.5 5.8 %all-to-all-start.1 = ((bf16[8,4,64,128]{3,2,1,0:T(8,128)(2,1)}), bf16[8,4,64,128]{3,2,1,0:T(8,128)(2,1)S(1)}, u32[]{:S(2)}, u32[]{:S(2)}) async-start(bf16[8,4,64,128]{3,2,1,0:T(8,128)(2,1)} %gather_far.1), calls=%async_computation.1 | async-start | bytes 1048576 | tf_op jit(solution)/shard_map/all_to_all | solution.py:537
  27.3 0.6 reshape.75.refs_9_
  27.9 0.6 reshape.74.refs_8_
  28.5 0.1 copy.21
  28.6 0.7 reshape.72.kept
  29.5 0.2 broadcast_in_dim.95
  29.7 0.8 %reshape.76.refs_10_.mask_in = f32[5,24,384]{2,1,0:T(8,128)} reshape(f32[5,24,6,64]{3,2,1,0:T(8,128)S(1)} %broadcast_in_dim.95) | data formatting | bytes 368640 | tf_op jit(solution)/shard_map/reshape | solution.py:543
  30.5 8.8 %near.1 = (bf16[1536,640]{1,0:T(8,128)(2,1)}, bf16[384,640]{1,0:T(8,128)(2,1)}, bf16[5,128,1536]{2,1,0:T(8,128)(2,1)}, bf16[5,128,1536]{2,1,0:T(8,128)(2,1)}, bf...) custom-call(f32[16,128]{1,0:T(8,128)} %copy-done.4, f32[16,128]{1,0:T(8,128)} %copy-done.8, f32[16,128]{1,0:T(8,128)} %copy-done.7, ...), custom_call_target="tpu_custom_call" | custom-call | tf_op jit(solution)/shard_map/near/pallas_call | solution.py:560
  39.4 1.7 %all-to-all-done.1.far_in = bf16[8,4,64,128]{3,2,1,0:T(8,128)(2,1)S(1)} async-done(((bf16[8,4,64,128]{3,2,1,0:T(8,128)(2,1)}), bf16[8,4,64,128]{3,2,1,0:T(8,128)(2,1)S(1)}, u32[]{:S(2)}, u32[]{:S(2)}) %all-to-all-start.1) | async-done | bytes 524320 | tf_op jit(solution)/shard_map/all_to_all | solution.py:537
  41.0 0.8 %copy-done.2 = bf16[8,4,64,128]{3,2,1,0:T(8,128)(2,1)} copy-done((bf16[8,4,64,128]{3,2,1,0:T(8,128)(2,1)}, bf16[8,4,64,128]{3,2,1,0:T(8,128)(2,1)S(1)}, u32[]{:S(2)}) %copy-start.2) | copy-done | bytes 524312
  41.9 11.9 %meet.1 = (bf16[384,640]{1,0:T(8,128)(2,1)}, bf16[5,1536,384]{2,1,0:T(8,128)(2,1)}, f32[5,8,384]{2,1,0:T(8,128)}, bf16[5,128,384]{2,1,0:T(8,128)(2,1)}, bf16[8,2...) custom-call(s32[6,60]{1,0:T(8,128)} %reshape.72.kept, s32[8,128]{1,0:T(8,128)} %copy-done.5, ...), custom_call_target="tpu_custom_call" | custom-call | tf_op jit(solution)/shard_map/meet/pallas_call | solution.py:594
  53.8 4.3 %all-to-all-start.2 = ((bf16[8,4,64,128]{3,2,1,0:T(8,128)(2,1)}), bf16[8,4,64,128]{3,2,1,0:T(8,128)(2,1)S(1)}, u32[]{:S(2)}, u32[]{:S(2)}) async-start(bf16[8,4,64,128]{3,2,1,0:T(8,128)(2,1)} %get-tuple-element.34), calls=%async_computation.2 | async-start | bytes 1048576 | tf_op jit(solution)/shard_map/all_to_all | solution.py:631
  58.2 12.1 %grad.1 = (bf16[384,640]{1,0:T(8,128)(2,1)}, bf16[1536,640]{1,0:T(8,128)(2,1)}, bf16[1536,640]{1,0:T(8,128)(2,1)}, f32[16,64,256]{2,1,0:T(8,128)}) custom-call(s32[6,60]{1,0:T(8,128)} %reshape.72.kept, s32[8,128]{1,0:T(8,128)} %copy-done.5, s32[8,128]{1,0:T(8,128)} %fusion.4.wanted, bf16[5,128,1536]{2,1,0:T(8,128)(2,1)} %get-tuple-element.28.kn_t_in, ...), custom_call_target="tpu_custom_call" | custom-call | tf_op jit(solution)/shard_map/grad/pallas_call | solution.py:633
  70.2 1.0 %all-to-all-done.2.back_in = bf16[8,4,64,128]{3,2,1,0:T(8,128)(2,1)S(1)} async-done(((bf16[8,4,64,128]{3,2,1,0:T(8,128)(2,1)}), bf16[8,4,64,128]{3,2,1,0:T(8,128)(2,1)S(1)}, u32[]{:S(2)}, u32[]{:S(2)}) %all-to-all-start.2) | async-done | bytes 524320 | tf_op jit(solution)/shard_map/all_to_all | solution.py:631
  71.3 1.2 %copy-done = f32[16,64,256]{2,1,0:T(8,128)S(1)} copy-done((f32[16,64,256]{2,1,0:T(8,128)S(1)}, f32[16,64,256]{2,1,0:T(8,128)}, u32[]{:S(2)}) %copy-start) | copy-done | bytes 1048600
  72.5 2.1 %finish.1 = (bf16[1536,640]{1,0:T(8,128)(2,1)}, bf16[1536,640]{1,0:T(8,128)(2,1)}) custom-call(s32[8,128]{1,0:T(8,128)S(1)} %copy-done.1, bf16[8,4,64,128]{3,2,1,0:T(8,128)(2,1)S(1)} %all-to-all-done.2.back_in, f32[16,64,256]{2,1,0:T(8,128)S(1)} %copy-done, bf16[1536,640]{1,0:T(8,128)(2,1)} %get-tuple-element.36.dk_in, ...), custom_call_target="tpu_custom_call", output_to_operand_aliasing={{0}: (3, {}), {1}: (4, {})} | custom-call | tf_op jit(solution)/shard_map/finish/pallas_call | solution.py:665
  (30 shorter events, 0.4 us)
Async XLA Ops:
  1.7 19.8 %copy-start.5 = (s32[8,128]{1,0:T(8,128)}, s32[8,128]{1,0:T(8,128)S(1)}, u32[]{:S(2)}) copy-start(s32[8,128]{1,0:T(8,128)S(1)} %broadcast_select_fusion.request) | copy-start | bytes 12292
  2.3 14.0 %all-to-all-start = ((s32[8,8,128]{2,1,0:T(8,128)}), s32[8,8,128]{2,1,0:T(8,128)S(1)}, u32[]{:S(2)}, u32[]{:S(2)}) async-start(s32[8,8,128]{2,1,0:T(8,128)} %broadcast_in_dim.96), calls=%async_computation | async-start | bytes 65536 | tf_op jit(solution)/shard_map/all_to_all | solution.py:499
  12.8 4.7 %copy-start.4 = (f32[16,128]{1,0:T(8,128)}, f32[16,128]{1,0:T(8,128)S(1)}, u32[]{:S(2)}) copy-start(f32[16,128]{1,0:T(8,128)S(1)} %maximum_bitcast_fusion.refs_0_) | copy-start | bytes 24580
  12.8 4.1 %collective-permute-start.2 = (f32[16,128]{1,0:T(8,128)S(1)}, f32[16,128]{1,0:T(8,128)S(1)}, u32[]{:S(2)}, u32[]{:S(2)}) collective-permute-start(f32[16,128]{1,0:T(8,128)S(1)} %maximum_bitcast_fusion.refs_0_), channel_id=1, source_target_pairs={{0,3},{1,0},{2,1},{3,2},{4,7},{5,4},{6,5},{7,6},{8,11},{9,8},{10,9... | collective-permute-start | bytes 24584 | tf_op jit(solution)/shard_map/ppermute | solution.py:515
  13.5 3.7 %collective-permute-start.1 = (f32[16,128]{1,0:T(8,128)S(1)}, f32[16,128]{1,0:T(8,128)S(1)}, u32[]{:S(2)}, u32[]{:S(2)}) collective-permute-start(f32[16,128]{1,0:T(8,128)S(1)} %maximum_bitcast_fusion.refs_0_), channel_id=1, source_target_pairs={{0,2},{1,3},{2,0},{3,1},{4,6},{5,7},{6,4},{7,5},{8,10},{9,11},{10,... | collective-permute-start | bytes 24584 | tf_op jit(solution)/shard_map/ppermute | solution.py:515
  14.4 3.1 %collective-permute-start = (f32[16,128]{1,0:T(8,128)S(1)}, f32[16,128]{1,0:T(8,128)S(1)}, u32[]{:S(2)}, u32[]{:S(2)}) collective-permute-start(f32[16,128]{1,0:T(8,128)S(1)} %maximum_bitcast_fusion.refs_0_), channel_id=1, source_target_pairs={{0,1},{1,2},{2,3},{3,0},{4,5},{5,6},{6,7},{7,4},{8,9},{9,10},{10,1... | collective-permute-start | bytes 24584 | tf_op jit(solution)/shard_map/ppermute | solution.py:515
  16.9 10.4 %copy-start.9 = (f32[640]{0:T(1024)S(1)}, f32[640]{0:T(1024)}, u32[]{:S(2)}) copy-start(f32[640]{0:T(1024)} %refs_4_.3) | copy-start | bytes 7684
  16.9 11.0 %copy-start.3 = (s32[6,5,12]{2,0,1:T(8,128)S(1)}, s32[6,5,12]{2,0,1:T(8,128)}, u32[]{:S(2)}) copy-start(s32[6,5,12]{2,0,1:T(8,128)} %param.13) | copy-start | bytes 4324
  16.9 11.0 %copy-start.10 = (f32[640]{0:T(1024)S(1)}, f32[640]{0:T(1024)}, u32[]{:S(2)}) copy-start(f32[640]{0:T(1024)} %param.10) | copy-start | bytes 7684
  16.9 0.6 copy-start.6
  17.2 0.6 copy-start.7
  17.8 0.6 copy-start.8
  21.5 19.5 %all-to-all-start.1 = ((bf16[8,4,64,128]{3,2,1,0:T(8,128)(2,1)}), bf16[8,4,64,128]{3,2,1,0:T(8,128)(2,1)S(1)}, u32[]{:S(2)}, u32[]{:S(2)}) async-start(bf16[8,4,64,128]{3,2,1,0:T(8,128)(2,1)} %gather_far.1), calls=%async_computation.1 | async-start | bytes 1048576 | tf_op jit(solution)/shard_map/all_to_all | solution.py:537
  41.0 0.8 %copy-start.2 = (bf16[8,4,64,128]{3,2,1,0:T(8,128)(2,1)}, bf16[8,4,64,128]{3,2,1,0:T(8,128)(2,1)S(1)}, u32[]{:S(2)}) copy-start(bf16[8,4,64,128]{3,2,1,0:T(8,128)(2,1)S(1)} %all-to-all-done.1.far_in) | copy-start | bytes 1572868
  53.8 17.5 %all-to-all-start.2 = ((bf16[8,4,64,128]{3,2,1,0:T(8,128)(2,1)}), bf16[8,4,64,128]{3,2,1,0:T(8,128)(2,1)S(1)}, u32[]{:S(2)}, u32[]{:S(2)}) async-start(bf16[8,4,64,128]{3,2,1,0:T(8,128)(2,1)} %get-tuple-element.34), calls=%async_computation.2 | async-start | bytes 1048576 | tf_op jit(solution)/shard_map/all_to_all | solution.py:631
  58.1 13.1 %copy-start.1 = (s32[8,128]{1,0:T(8,128)S(1)}, s32[8,128]{1,0:T(8,128)}, u32[]{:S(2)}) copy-start(s32[8,128]{1,0:T(8,128)} %fusion.4.wanted) | copy-start | bytes 12292
  71.3 1.2 %copy-start = (f32[16,64,256]{2,1,0:T(8,128)S(1)}, f32[16,64,256]{2,1,0:T(8,128)}, u32[]{:S(2)}) copy-start(f32[16,64,256]{2,1,0:T(8,128)} %get-tuple-element.35.tiles) | copy-start | bytes 3145732

commit v5 on v4

--- a/solution.py
+++ b/solution.py
@@ -497,7 +497,7 @@
     lane = jnp.arange(HD, dtype=jnp.int32)[None, :]
     request = jnp.where(lane == 0, low[:, None], high[:, None])
     wanted = lax.all_to_all(
-        jnp.broadcast_to(request[:, None], (slab_count, 8, HD)),
+        jnp.broadcast_to(request[:, None], (slab_count, 4, HD)),
         "slab", split_axis=0, concat_axis=0, tiled=True,
     )[:, 0]
     wanted = jnp.where(wanted == 0, 0, jnp.where(lane == 0, LIMIT - wanted, wanted - 1))

time: 75.6 us -> 75.6 us (level)
  no operation moved by 1% of the time
where the time goes in v5:
time: 75.6 us; the launch traced here: 74.7 us
  Pallas kernels  38 us (50%)
  starting transfers between devices  19.1 us (25%)
  local copies, waits for them, and re-layouts  6.62 us (9%)
  waiting for transfers between devices  5.03 us (7%)
  other arithmetic  4.95 us (7%)
  between operations  0.94 us (1%)
    pallas_call x1, Pallas kernels, local(): pl.pallas_call(functools.partial(grad_kernel, head_step), in_specs=[SMEM]...  12.1 us
    pallas_call x1, Pallas kernels, local(): pl.pallas_call(functools.partial(meet_kernel, head_step), in_specs=[SMEM]...  11.9 us
    pallas_call x1, Pallas kernels, local(): pl.pallas_call(functools.partial(near_kernel, full_width, group_count), g...  8.85 us
    all_to_all x1, starting transfers between devices, local(): lax.all_to_all(jnp.broadcast_to(request[:, None], (slab_count, 4, HD)), '...  7.28 us
    all_to_all x1, starting transfers between devices, local(): lax.all_to_all(outgoing, 'slab', split_axis=0, concat_axis=0, tiled=True)  5.74 us
    all_to_all x1, starting transfers between devices, local(): lax.all_to_all(far_grad, 'slab', split_axis=0, concat_axis=0, tiled=True)  4.33 us
    pallas_call x1, Pallas kernels, local(): pl.pallas_call(functools.partial(gather_kernel, full_width, head_step, gr...  3.14 us
    unnamed x23, local copies, waits for them, and re-layouts  2.95 us
  transfers between devices with their start and end apart: 6, of which 5 were waited for; matrix products, arithmetic and copies ran while one was open for 9% of the time, Pallas kernels for 28%

profile of v5, /device:TPU:0, one launch (start us, length us, event | category | flops | bytes accessed | tf_op | source)
XLA Modules:
  0.0 74.7 jit_solution(14000853230448418944)
XLA Ops:
  0.7 0.7 broadcast_add_fusion
  1.4 0.2 select_reduce_fusion.1
  1.7 0.6 broadcast_in_dim.96
  2.3 7.3 %all-to-all-start = ((s32[8,4,128]{2,1,0:T(4,128)}), s32[8,4,128]{2,1,0:T(4,128)S(1)}, u32[]{:S(2)}, u32[]{:S(2)}) async-start(s32[8,4,128]{2,1,0:T(4,128)} %broadcast_in_dim.96), calls=%async_computation | async-start | bytes 32768 | tf_op jit(solution)/shard_map/all_to_all | solution.py:499
  9.6 1.2 %multiply_reduce_fusion.1 = f32[384]{0:T(512)S(1)} fusion(bf16[384,640]{1,0:T(8,128)(2,1)} %refs_4_.2), kind=kLoop, calls=%fused_computation.1 | loop fusion | flops 736896 | bytes 493056 | tf_op jit(solution)/shard_map/reduce_sum | solution.py:509
  10.8 2.0 %multiply_reduce_fusion = f32[1536]{0:T(1024)S(1)} fusion(bf16[1536,640]{1,0:T(8,128)(2,1)} %refs_5_.3), kind=kLoop, calls=%fused_computation | loop fusion | flops 2947584 | bytes 1972224 | tf_op jit(solution)/shard_map/reduce_sum | solution.py:508
  12.8 0.7 collective-permute-start.2
  13.5 0.9 %collective-permute-start.1 = (f32[16,128]{1,0:T(8,128)S(1)}, f32[16,128]{1,0:T(8,128)S(1)}, u32[]{:S(2)}, u32[]{:S(2)}) collective-permute-start(f32[16,128]{1,0:T(8,128)S(1)} %maximum_bitcast_fusion.refs_0_), channel_id=1, source_target_pairs={{0,2},{1,3},{2,0},{3,1},{4,6},{5,7},{6,4},{7,5},{8,10},{9,11},{10,... | collective-permute-start | bytes 24584 | tf_op jit(solution)/shard_map/ppermute | solution.py:515
  14.4 0.2 collective-permute-start
  14.6 1.5 %all-to-all-done = s32[8,4,128]{2,1,0:T(4,128)S(1)} async-done(((s32[8,4,128]{2,1,0:T(4,128)}), s32[8,4,128]{2,1,0:T(4,128)S(1)}, u32[]{:S(2)}, u32[]{:S(2)}) %all-to-all-start) | async-done | bytes 16416 | tf_op jit(solution)/shard_map/all_to_all | solution.py:499
  16.1 0.6 fusion.4.wanted
  16.8 0.4 collective-permute-done.1.refs_2_
  17.2 0.3 collective-permute-done.refs_1_
  17.5 0.2 copy-done.7
  17.7 0.6 copy-done.8
  18.3 3.1 %gather_far.1 = bf16[8,4,64,128]{3,2,1,0:T(8,128)(2,1)} custom-call(s32[8,128]{1,0:T(8,128)} %fusion.4.wanted, f32[16,128]{1,0:T(8,128)} %copy-done.4, f32[16,128]{1,0:T(8,128)} %copy-done.8, f32[16,128]{1,0:T(8,128)} %copy-done.7, f32[16,128]{1,0:T(8,128)} %copy-done.6, f32[640]{0:T(1024)} %refs_4_.3, bf16[1536,640]{1,0:T(8,128)(2,1)} %refs_5_.3, ...), custom_call_target="tpu_custom_call" | custom-call | tf_op jit(solution)/shard_map/gather_far/pallas_call | solution.py:522
  21.5 5.7 %all-to-all-start.1 = ((bf16[8,4,64,128]{3,2,1,0:T(8,128)(2,1)}), bf16[8,4,64,128]{3,2,1,0:T(8,128)(2,1)S(1)}, u32[]{:S(2)}, u32[]{:S(2)}) async-start(bf16[8,4,64,128]{3,2,1,0:T(8,128)(2,1)} %gather_far.1), calls=%async_computation.1 | async-start | bytes 1048576 | tf_op jit(solution)/shard_map/all_to_all | solution.py:537
  27.2 0.6 reshape.75.refs_9_
  27.9 0.6 reshape.74.refs_8_
  28.4 0.1 copy.21
  28.6 0.7 reshape.72.kept
  29.5 0.2 broadcast_in_dim.95
  29.7 0.8 %reshape.76.refs_10_.mask_in = f32[5,24,384]{2,1,0:T(8,128)} reshape(f32[5,24,6,64]{3,2,1,0:T(8,128)S(1)} %broadcast_in_dim.95) | data formatting | bytes 368640 | tf_op jit(solution)/shard_map/reshape | solution.py:543
  30.5 8.8 %near.1 = (bf16[1536,640]{1,0:T(8,128)(2,1)}, bf16[384,640]{1,0:T(8,128)(2,1)}, bf16[5,128,1536]{2,1,0:T(8,128)(2,1)}, bf16[5,128,1536]{2,1,0:T(8,128)(2,1)}, bf...) custom-call(f32[16,128]{1,0:T(8,128)} %copy-done.4, f32[16,128]{1,0:T(8,128)} %copy-done.8, f32[16,128]{1,0:T(8,128)} %copy-done.7, ...), custom_call_target="tpu_custom_call" | custom-call | tf_op jit(solution)/shard_map/near/pallas_call | solution.py:560
  39.3 1.7 %all-to-all-done.1.far_in = bf16[8,4,64,128]{3,2,1,0:T(8,128)(2,1)S(1)} async-done(((bf16[8,4,64,128]{3,2,1,0:T(8,128)(2,1)}), bf16[8,4,64,128]{3,2,1,0:T(8,128)(2,1)S(1)}, u32[]{:S(2)}, u32[]{:S(2)}) %all-to-all-start.1) | async-done | bytes 524320 | tf_op jit(solution)/shard_map/all_to_all | solution.py:537
  41.0 0.8 %copy-done.2 = bf16[8,4,64,128]{3,2,1,0:T(8,128)(2,1)} copy-done((bf16[8,4,64,128]{3,2,1,0:T(8,128)(2,1)}, bf16[8,4,64,128]{3,2,1,0:T(8,128)(2,1)S(1)}, u32[]{:S(2)}) %copy-start.2) | copy-done | bytes 524312
  41.9 11.9 %meet.1 = (bf16[384,640]{1,0:T(8,128)(2,1)}, bf16[5,1536,384]{2,1,0:T(8,128)(2,1)}, f32[5,8,384]{2,1,0:T(8,128)}, bf16[5,128,384]{2,1,0:T(8,128)(2,1)}, bf16[8,2...) custom-call(s32[6,60]{1,0:T(8,128)} %reshape.72.kept, s32[8,128]{1,0:T(8,128)} %copy-done.5, ...), custom_call_target="tpu_custom_call" | custom-call | tf_op jit(solution)/shard_map/meet/pallas_call | solution.py:594
  53.8 4.3 %all-to-all-start.2 = ((bf16[8,4,64,128]{3,2,1,0:T(8,128)(2,1)}), bf16[8,4,64,128]{3,2,1,0:T(8,128)(2,1)S(1)}, u32[]{:S(2)}, u32[]{:S(2)}) async-start(bf16[8,4,64,128]{3,2,1,0:T(8,128)(2,1)} %get-tuple-element.34), calls=%async_computation.2 | async-start | bytes 1048576 | tf_op jit(solution)/shard_map/all_to_all | solution.py:631
  58.1 12.1 %grad.1 = (bf16[384,640]{1,0:T(8,128)(2,1)}, bf16[1536,640]{1,0:T(8,128)(2,1)}, bf16[1536,640]{1,0:T(8,128)(2,1)}, f32[16,64,256]{2,1,0:T(8,128)}) custom-call(s32[6,60]{1,0:T(8,128)} %reshape.72.kept, s32[8,128]{1,0:T(8,128)} %copy-done.5, s32[8,128]{1,0:T(8,128)} %fusion.4.wanted, bf16[5,128,1536]{2,1,0:T(8,128)(2,1)} %get-tuple-element.28.kn_t_in, ...), custom_call_target="tpu_custom_call" | custom-call | tf_op jit(solution)/shard_map/grad/pallas_call | solution.py:633
  70.2 1.0 %all-to-all-done.2.back_in = bf16[8,4,64,128]{3,2,1,0:T(8,128)(2,1)S(1)} async-done(((bf16[8,4,64,128]{3,2,1,0:T(8,128)(2,1)}), bf16[8,4,64,128]{3,2,1,0:T(8,128)(2,1)S(1)}, u32[]{:S(2)}, u32[]{:S(2)}) %all-to-all-start.2) | async-done | bytes 524320 | tf_op jit(solution)/shard_map/all_to_all | solution.py:631
  71.3 1.2 %copy-done = f32[16,64,256]{2,1,0:T(8,128)S(1)} copy-done((f32[16,64,256]{2,1,0:T(8,128)S(1)}, f32[16,64,256]{2,1,0:T(8,128)}, u32[]{:S(2)}) %copy-start) | copy-done | bytes 1048600
  72.5 2.0 %finish.1 = (bf16[1536,640]{1,0:T(8,128)(2,1)}, bf16[1536,640]{1,0:T(8,128)(2,1)}) custom-call(s32[8,128]{1,0:T(8,128)S(1)} %copy-done.1, bf16[8,4,64,128]{3,2,1,0:T(8,128)(2,1)S(1)} %all-to-all-done.2.back_in, f32[16,64,256]{2,1,0:T(8,128)S(1)} %copy-done, bf16[1536,640]{1,0:T(8,128)(2,1)} %get-tuple-element.36.dk_in, ...), custom_call_target="tpu_custom_call", output_to_operand_aliasing={{0}: (3, {}), {1}: (4, {})} | custom-call | tf_op jit(solution)/shard_map/finish/pallas_call | solution.py:665
  (30 shorter events, 0.4 us)
Async XLA Ops:
  1.7 19.8 %copy-start.5 = (s32[8,128]{1,0:T(8,128)}, s32[8,128]{1,0:T(8,128)S(1)}, u32[]{:S(2)}) copy-start(s32[8,128]{1,0:T(8,128)S(1)} %broadcast_select_fusion.request) | copy-start | bytes 12292
  2.3 13.9 %all-to-all-start = ((s32[8,4,128]{2,1,0:T(4,128)}), s32[8,4,128]{2,1,0:T(4,128)S(1)}, u32[]{:S(2)}, u32[]{:S(2)}) async-start(s32[8,4,128]{2,1,0:T(4,128)} %broadcast_in_dim.96), calls=%async_computation | async-start | bytes 32768 | tf_op jit(solution)/shard_map/all_to_all | solution.py:499
  12.8 4.7 %copy-start.4 = (f32[16,128]{1,0:T(8,128)}, f32[16,128]{1,0:T(8,128)S(1)}, u32[]{:S(2)}) copy-start(f32[16,128]{1,0:T(8,128)S(1)} %maximum_bitcast_fusion.refs_0_) | copy-start | bytes 24580
  12.8 3.9 %collective-permute-start.2 = (f32[16,128]{1,0:T(8,128)S(1)}, f32[16,128]{1,0:T(8,128)S(1)}, u32[]{:S(2)}, u32[]{:S(2)}) collective-permute-start(f32[16,128]{1,0:T(8,128)S(1)} %maximum_bitcast_fusion.refs_0_), channel_id=1, source_target_pairs={{0,3},{1,0},{2,1},{3,2},{4,7},{5,4},{6,5},{7,6},{8,11},{9,8},{10,9... | collective-permute-start | bytes 24584 | tf_op jit(solution)/shard_map/ppermute | solution.py:515
  13.5 3.7 %collective-permute-start.1 = (f32[16,128]{1,0:T(8,128)S(1)}, f32[16,128]{1,0:T(8,128)S(1)}, u32[]{:S(2)}, u32[]{:S(2)}) collective-permute-start(f32[16,128]{1,0:T(8,128)S(1)} %maximum_bitcast_fusion.refs_0_), channel_id=1, source_target_pairs={{0,2},{1,3},{2,0},{3,1},{4,6},{5,7},{6,4},{7,5},{8,10},{9,11},{10,... | collective-permute-start | bytes 24584 | tf_op jit(solution)/shard_map/ppermute | solution.py:515
  14.4 3.1 %collective-permute-start = (f32[16,128]{1,0:T(8,128)S(1)}, f32[16,128]{1,0:T(8,128)S(1)}, u32[]{:S(2)}, u32[]{:S(2)}) collective-permute-start(f32[16,128]{1,0:T(8,128)S(1)} %maximum_bitcast_fusion.refs_0_), channel_id=1, source_target_pairs={{0,1},{1,2},{2,3},{3,0},{4,5},{5,6},{6,7},{7,4},{8,9},{9,10},{10,1... | collective-permute-start | bytes 24584 | tf_op jit(solution)/shard_map/ppermute | solution.py:515
  16.7 10.5 %copy-start.9 = (f32[640]{0:T(1024)S(1)}, f32[640]{0:T(1024)}, u32[]{:S(2)}) copy-start(f32[640]{0:T(1024)} %refs_4_.3) | copy-start | bytes 7684
  16.7 11.1 %copy-start.3 = (s32[6,5,12]{2,0,1:T(8,128)S(1)}, s32[6,5,12]{2,0,1:T(8,128)}, u32[]{:S(2)}) copy-start(s32[6,5,12]{2,0,1:T(8,128)} %param.13) | copy-start | bytes 4324
  16.7 11.1 %copy-start.10 = (f32[640]{0:T(1024)S(1)}, f32[640]{0:T(1024)}, u32[]{:S(2)}) copy-start(f32[640]{0:T(1024)} %param.10) | copy-start | bytes 7684
  16.7 0.8 %copy-start.6 = (f32[16,128]{1,0:T(8,128)}, f32[16,128]{1,0:T(8,128)S(1)}, u32[]{:S(2)}) copy-start(f32[16,128]{1,0:T(8,128)S(1)} %collective-permute-done.2.refs_3_) | copy-start | bytes 24580
  17.2 0.6 copy-start.7
  17.7 0.6 copy-start.8
  21.5 19.5 %all-to-all-start.1 = ((bf16[8,4,64,128]{3,2,1,0:T(8,128)(2,1)}), bf16[8,4,64,128]{3,2,1,0:T(8,128)(2,1)S(1)}, u32[]{:S(2)}, u32[]{:S(2)}) async-start(bf16[8,4,64,128]{3,2,1,0:T(8,128)(2,1)} %gather_far.1), calls=%async_computation.1 | async-start | bytes 1048576 | tf_op jit(solution)/shard_map/all_to_all | solution.py:537
  41.0 0.8 %copy-start.2 = (bf16[8,4,64,128]{3,2,1,0:T(8,128)(2,1)}, bf16[8,4,64,128]{3,2,1,0:T(8,128)(2,1)S(1)}, u32[]{:S(2)}) copy-start(bf16[8,4,64,128]{3,2,1,0:T(8,128)(2,1)S(1)} %all-to-all-done.1.far_in) | copy-start | bytes 1572868
  53.8 17.5 %all-to-all-start.2 = ((bf16[8,4,64,128]{3,2,1,0:T(8,128)(2,1)}), bf16[8,4,64,128]{3,2,1,0:T(8,128)(2,1)S(1)}, u32[]{:S(2)}, u32[]{:S(2)}) async-start(bf16[8,4,64,128]{3,2,1,0:T(8,128)(2,1)} %get-tuple-element.34), calls=%async_computation.2 | async-start | bytes 1048576 | tf_op jit(solution)/shard_map/all_to_all | solution.py:631
  58.1 13.2 %copy-start.1 = (s32[8,128]{1,0:T(8,128)S(1)}, s32[8,128]{1,0:T(8,128)}, u32[]{:S(2)}) copy-start(s32[8,128]{1,0:T(8,128)} %fusion.4.wanted) | copy-start | bytes 12292
  71.3 1.2 %copy-start = (f32[16,64,256]{2,1,0:T(8,128)S(1)}, f32[16,64,256]{2,1,0:T(8,128)}, u32[]{:S(2)}) copy-start(f32[16,64,256]{2,1,0:T(8,128)} %get-tuple-element.35.tiles) | copy-start | bytes 3145732
